TPU v7x, 256 devices: a whole 4x4x8 slice. The times are simulated.
256 devices in a mesh: noise: 8 (over x, y_hi), row: 4 (over y_lo, core), col: 8 (over z).
Axes of the slice: x: 4, y: 4 (y_hi: 2, y_lo: 2; y = y_hi * 2 + y_lo), z: 8, core: 2. Of those that a mesh axis runs over, the one named last changes fastest.
Arguments:
- image: bfloat16 [1024, 256, 128], P(('noise', 'row'), 'col'), parts along dimension 0, may hold values from -6 to 6
- noise_level: int32 [8], P('noise'), parts along dimension 0, may hold values from 0 to 7
- cond_table: float32 [8, 256], replicated, may hold values from -6 to 6
- ada_fine: float32 [256, 128], replicated, may hold values from -0.375 to 0.375
- fine_qkv: bfloat16 [128, 384], replicated, may hold values from -0.5 to 0.5
- fine_scale: float32 [2], replicated, may hold values from 4 to 16
- fine_out_w: bfloat16 [128, 128], replicated, may hold values from -0.5 to 0.5
- fine_post: float32 [128], replicated, may hold values from 0.1 to 1.9
- merge_w: bfloat16 [512, 256], replicated, may hold values from -0.25 to 0.25
- coarse_in_w: bfloat16 [256, 1024], replicated, may hold values from -0.375 to 0.375
- ada_coarse: float32 [256, 1024], replicated, may hold values from -0.375 to 0.375
- coarse_qkv: bfloat16 [3, 1024, 1024], P(None, None, 'col'), may hold values from -0.1875 to 0.1875
- coarse_scale: float32 [16], P('col'), may hold values from 4 to 16
- coarse_out_w: bfloat16 [1024, 1024], P('col'), may hold values from -0.1875 to 0.1875
- coarse_post: float32 [1024], replicated, may hold values from 0.1 to 1.9
Outputs:
- fine_out: bfloat16 [1024, 256, 128], P(('noise', 'row'), 'col'), parts along dimension 0
- coarse_out: bfloat16 [64, 16, 1024], P(('noise', 'row'), 'col'), parts along dimension 0
There are 8 independent parts, one for each index of `noise`. A program takes and returns all parts, laid end to end along the dimension named above; an argument that names none is the same for every part. Nothing has to cross between parts.
All inputs are finite; a program needn't handle non-finite values.
Results may differ from a plain program's by a relative error of at most 0.035.
Values may be sent and summed in bfloat16 or wider, within the bound.
No kernel may reach another device: no remote copies, remote signals or barrier semaphores. Data moves between devices by JAX's collectives and lax.ppermute only.
A program may use at most 128 MiB of HBM per device.

v0:
```python
import jax
import jax.numpy as jnp
from jax import lax
from jax.sharding import PartitionSpec as P

HEAD = 64
TILE = 32
POOL = 8


def with_halo(x, sides, width):
    for axis, dim in sides:
        devices, length = (lax.axis_size(axis), x.shape[dim])
        up = [(i, (i + 1) % devices) for i in range(devices - 1)]
        down = [(j, i) for i, j in up]
        last = lax.slice_in_dim(x, length - width, length, axis=dim)
        initial = lax.slice_in_dim(x, 0, width, axis=dim)
        before = lax.ppermute(last, axis, up)
        after = lax.ppermute(initial, axis, down)
        x = jnp.concatenate([before, x, after], axis=dim)
    return x


def rms(value):
    return value * lax.rsqrt(jnp.mean(value * value, axis=-1, keepdims=True) + 1e-06)


def cosine(value, heads):
    shaped = value.reshape(value.shape[:-1] + (heads, HEAD))
    return rms(shaped).reshape(value.shape)


def attend(queries, keys, values, valid, scale, heads):
    results = []
    for head in range(heads):
        low = head * HEAD
        scores = jnp.dot(
            queries[:, low : low + HEAD],
            keys[:, low : low + HEAD].T,
            preferred_element_type=jnp.float32,
        )
        scores = scores * (scale[head] / HEAD)
        if valid is not None:
            scores = jnp.where(valid[None, :], scores, -jnp.inf)
        top = jnp.max(scores, axis=-1, keepdims=True)
        expo = jnp.exp(scores - top)
        if valid is not None:
            expo = jnp.where(valid[None, :], expo, 0.0)
        weights = (expo / jnp.sum(expo, axis=-1, keepdims=True)).astype(jnp.bfloat16)
        results.append(
            jnp.dot(weights, values[:, low : low + HEAD], preferred_element_type=jnp.float32)
        )
    return jnp.concatenate(results, axis=-1).astype(jnp.bfloat16)


def attend_blocks(queries, keys, values, valid, scale, heads):
    count, width = queries.shape
    block = min(512, count)
    grouped = queries.reshape(count // block, block, width)

    def one_block(part_q):
        return attend(part_q, keys, values, valid, scale, heads)

    return lax.map(one_block, grouped).reshape(count, width)


def body(
    image,
    noise_level,
    cond_table,
    ada_fine,
    fine_qkv,
    fine_scale,
    fine_out_w,
    fine_post,
    merge_w,
    coarse_in_w,
    ada_coarse,
    coarse_qkv,
    coarse_scale,
    coarse_out_w,
    coarse_post,
):
    highest = lax.Precision.HIGHEST
    tile = TILE
    rows_loc, cols_loc, width = image.shape
    heads = width // HEAD
    levels = jnp.arange(cond_table.shape[0], dtype=jnp.int32)
    hot = (levels == noise_level[0]).astype(jnp.float32)
    cond = jnp.dot(hot, cond_table, precision=highest)
    fine_gain = 1.0 + jnp.dot(cond, ada_fine, precision=highest)
    coarse_gain = 1.0 + jnp.dot(cond, ada_coarse, precision=highest)
    xfull = image.astype(jnp.float32)
    xn = (rms(xfull) * fine_gain).astype(jnp.bfloat16)
    qproj = jnp.dot(xn.reshape(-1, width), fine_qkv[:, :width], preferred_element_type=jnp.float32)
    queries = cosine(qproj, heads).astype(jnp.bfloat16).reshape(rows_loc, cols_loc, width)
    shape = xn.shape[:2]
    proj = jnp.dot(xn.reshape(-1, width), fine_qkv[:, width:], preferred_element_type=jnp.float32)
    proj = proj.reshape(shape + (2 * width,))
    keys_out = cosine(proj[..., :width], heads).astype(jnp.bfloat16)
    values_out = proj[..., width:].astype(jnp.bfloat16)
    both = jnp.stack([keys_out, values_out], axis=0)
    padded = with_halo(both, (("row", 1), ("col", 2)), tile)
    keys_pad = padded[0]
    values_pad = padded[1]
    grid_rows = rows_loc * lax.axis_size("row")
    grid_cols = cols_loc * lax.axis_size("col")
    row_ids = (
        lax.axis_index("row") * rows_loc - tile + jnp.arange(rows_loc + 2 * tile, dtype=jnp.int32)
    )
    col_ids = (
        lax.axis_index("col") * cols_loc - tile + jnp.arange(cols_loc + 2 * tile, dtype=jnp.int32)
    )
    row_ok = (row_ids >= 0) & (row_ids < grid_rows)
    col_ok = (col_ids >= 0) & (col_ids < grid_cols)
    q_tile = queries.reshape(tile * tile, width)
    k_win = keys_pad.reshape(-1, width)
    v_win = values_pad.reshape(-1, width)
    valid = (row_ok[:, None] & col_ok[None, 0 : 3 * tile]).reshape(-1)
    result = attend_blocks(q_tile, k_win, v_win, valid, fine_scale, heads)
    pieces = [result.reshape(tile, tile, width)]
    attended = jnp.concatenate(pieces, axis=1)
    branch = jnp.dot(attended.reshape(-1, width), fine_out_w, preferred_element_type=jnp.float32)
    branch = branch.reshape(rows_loc, cols_loc, width)
    fine_out = (xfull + rms(branch) * fine_post).astype(jnp.bfloat16)
    merge_width = merge_w.shape[1]
    blocks = (
        fine_out.reshape(rows_loc // 2, 2, cols_loc // 2, 2, width)
        .transpose(0, 2, 1, 3, 4)
        .reshape(-1, 4 * width)
    )
    merged = jnp.dot(blocks, merge_w, preferred_element_type=jnp.float32).astype(jnp.bfloat16)
    pool_rows = rows_loc // (2 * POOL)
    pool_cols = cols_loc // (2 * POOL)
    merged = merged.reshape(pool_rows, POOL, pool_cols, POOL, merge_width).astype(jnp.float32)
    pooled = jnp.mean(merged, axis=(1, 3)).astype(jnp.bfloat16).reshape(-1, merge_width)
    coarse_in = jnp.dot(pooled, coarse_in_w, preferred_element_type=jnp.float32)
    cn = (rms(coarse_in) * coarse_gain).astype(jnp.bfloat16)
    coarse_width = cn.shape[1]
    local_width = coarse_qkv.shape[2]
    local_heads = local_width // HEAD
    proj = jnp.einsum(
        "nd,kde->kne",
        lax.all_gather(cn, ("row", "col"), axis=0, tiled=True),
        coarse_qkv,
        preferred_element_type=jnp.float32,
    )
    q_part = cosine(proj[0], local_heads)
    k_part = cosine(proj[1], local_heads)
    projected = jnp.concatenate([q_part, k_part, proj[2]], axis=-1).astype(jnp.bfloat16)
    own_count = cn.shape[0]
    row_count = own_count * lax.axis_size("col")
    row_start = lax.axis_index("row") * row_count
    q_rows = lax.dynamic_slice_in_dim(projected[:, :local_width], row_start, row_count, 0)
    k_all = projected[:, local_width : 2 * local_width]
    v_all = projected[:, 2 * local_width :]
    coarse_attended = attend(q_rows, k_all, v_all, None, coarse_scale, local_heads)
    coarse_branch = lax.psum_scatter(
        jnp.dot(coarse_attended, coarse_out_w, preferred_element_type=jnp.float32).astype(
            jnp.bfloat16
        ),
        "col",
        scatter_dimension=0,
        tiled=True,
    ).astype(jnp.float32)
    coarse_out = (coarse_in + rms(coarse_branch) * coarse_post).astype(jnp.bfloat16)
    coarse_out = coarse_out.reshape(pool_rows, pool_cols, coarse_width)
    return (fine_out, coarse_out)


def solution(mesh):
    in_specs = (
        P(("noise", "row"), "col", None),
        P("noise"),
        P(),
        P(),
        P(),
        P(),
        P(),
        P(),
        P(),
        P(),
        P(),
        P(None, None, "col"),
        P("col"),
        P("col", None),
        P(),
    )
    out_specs = (P(("noise", "row"), "col", None), P(("noise", "row"), "col", None))
    return jax.shard_map(body, mesh=mesh, in_specs=in_specs, out_specs=out_specs, check_vma=False)
```

profile of v0, /device:TPU:2, one launch (start us, length us, event | category | flops | bytes accessed | tf_op | source)
XLA Modules:
  0.0 353.1 jit_solution(10420121565007312929)
XLA Ops:
  8.0 1.2 fusion.33
  9.1 0.8 convolution_bitcast_fusion
  9.9 1.1 fusion.32
  11.0 1.2 fusion.35
  12.2 1.2 fusion.41
  13.5 0.8 slice_multiply_fusion
  14.3 1.7 mul.196
  16.0 1.9 reduce_sum.123
  17.9 1.3 copy.37
  19.3 1.1 copy.38
  20.3 2.2 mul.197
  22.5 1.4 mul.198
  23.9 1.1 fusion.37
  25.1 1.8 collective-permute-start
  26.9 1.3 collective-permute-start.1
  28.4 3.6 %collective-permute-done.1 = bf16[2,32,32,128]{3,2,1,0:T(8,128)(2,1)S(1)} collective-permute-done((bf16[2,32,32,128]{3,2,1,0:T(8,128)(2,1)S(1)}, bf16[2,32,32,128]{3,2,1,0:T(8,128)(2,1)S(1)}, u32[]{:S(2)}, u32[]{:S(2)}) %collective-permute-start.1) | collective-permute-done | bytes 524320 | tf_op jit(solution)/shard_map/ppermute | solution.py:19
  32.0 1.3 pad_maximum_fusion.2
  33.3 5.0 %collective-permute-start.2 = (bf16[2,96,32,128]{3,2,1,0:T(8,128)(2,1)}, bf16[2,96,32,128]{3,2,1,0:T(8,128)(2,1)}, u32[]{:S(2)}, u32[]{:S(2)}) collective-permute-start(bf16[2,96,32,128]{3,2,1,0:T(8,128)(2,1)} %pad_maximum_fusion.2), channel_id=1, source_target_pairs={{0,1},{1,2},{2,3},{3,4},{4,5},{5,6},{6,7},{8,9},{9,10},{10,11},{11... | collective-permute-start | bytes 4718600 | tf_op jit(solution)/shard_map/ppermute | solution.py:18
  38.3 1.3 collective-permute-start.3
  39.6 0.8 slice_bitcast_fusion.1
  40.5 1.2 multiply_reduce_fusion.1
  41.9 0.9 copy.39
  44.7 2.3 copy.42
  50.1 15.4 %collective-permute-done.2 = bf16[2,96,32,128]{3,2,1,0:T(8,128)(2,1)} collective-permute-done((bf16[2,96,32,128]{3,2,1,0:T(8,128)(2,1)}, bf16[2,96,32,128]{3,2,1,0:T(8,128)(2,1)}, u32[]{:S(2)}, u32[]{:S(2)}) %collective-permute-start.2) | collective-permute-done | bytes 1572896 | tf_op jit(solution)/shard_map/ppermute | solution.py:18
  65.6 5.8 %collective-permute-done.3 = bf16[2,96,32,128]{3,2,1,0:T(8,128)(2,1)} collective-permute-done((bf16[2,96,32,128]{3,2,1,0:T(8,128)(2,1)}, bf16[2,96,32,128]{3,2,1,0:T(8,128)(2,1)}, u32[]{:S(2)}, u32[]{:S(2)}) %collective-permute-start.3) | collective-permute-done | bytes 1572896 | tf_op jit(solution)/shard_map/ppermute | solution.py:19
  71.4 8.8 %pad_maximum_fusion.1 = bf16[2,96,96,128]{3,2,1,0:T(8,128)(2,1)S(1)} fusion(bf16[2,96,32,128]{3,2,1,0:T(8,128)(2,1)} %collective-permute-done.3, bf16[2,32,32,128]{3,2,1,0:T(8,128)(2,1)S(1)} %collective-permute-done.1, bf16[1,32,32,128]{3,2,1,0:T(8,128)(2,1)S(1)} %fusion.38, bf16[1,32,32,128]{3,2,1,0:T(8,128)(2,1)S(1)} %fusion.37, ...), kind=kLoop, calls=%fused_computation.33 | loop fusion | flops 28311552 | bytes 9437184 | tf_op jit(solution)/shard_map/concatenate | solution.py:20
  80.2 2.2 fusion.72
  82.5 118.6 %while.13 = (s32[]{:T(128)}, bf16[2,512,128]{2,1,0:T(8,128)(2,1)}, bf16[2,512,128]{2,1,0:T(8,128)(2,1)S(1)}, bf16[9216,128]{1,0:T(8,128)(2,1)S(1)}, f32[]{:T(128...) while((s32[]{:T(128)}, bf16[2,512,128]{2,1,0:T(8,128)(2,1)}, ...), condition=%wide.region_8.9_spmd.clone, body=%wide.region_3.8_spmd.clone.sunk | while | flops 2548374528 | bytes 133657432 | solution.py:64
  82.9 7.8 %fusion.104 = (f32[512]{0:T(512)S(1)}, f32[512,9216]{1,0:T(8,128)}) fusion(f32[]{:T(128)} %get-tuple-element.291, pred[9216]{0:T(1024)(128)(4,1)S(1)} %broadcast_in_dim.143, bf16[9216,128]{1,0:T(8,128)(2,1)S(1)} %get-tuple-element.290, bf16[512,128]{1,0:T(8,128)(2,1)S(1)} %dynamic-slice_bitcast_fusion.2), kind=kOutput, calls=%fused_computation.7.clone.1 | convolution fusion | flops 618135040 | bytes 21376004 | tf_op jit(solution)/shard_map/while/body/eval_jaxpr/dot_general | solution.py:37
  90.7 18.1 %fusion.105 = (f32[512]{0:T(512)S(1)}, f32[512]{0:T(512)S(1)}, f32[512,9216]{1,0:T(8,128)}) fusion(f32[512,9216]{1,0:T(8,128)} %get-tuple-element.262, f32[512]{0:T(512)S(1)} %get-tuple-element.263, f32[]{:T(128)} %get-tuple-element.291, pred[9216]{0:T(1024)(128)(4,1)S(1)} %broadcast_in_dim.143, f32[]{:T(128)} %get-tuple-element.293, ...), kind=kOutput, calls=%fused_computation.9.clone.1 | convolution fusion | flops 641727488 | bytes 40254472 | tf_op jit(solution)/shard_map/while/body/eval_jaxpr/dot_general | solution.py:37
  108.9 9.4 %fusion.108 = bf16[1,512,64]{1,2,0:T(8,128)(2,1)S(1)} fusion(bf16[9216,128]{1,0:T(8,128)(2,1)S(1)} %copy-done.4, f32[512,9216]{1,0:T(8,128)} %get-tuple-element.262, f32[512]{0:T(512)S(1)} %get-tuple-element.266, f32[512]{0:T(512)S(1)} %get-tuple-element.263, f32[]{:T(128)} %get-tuple-element.291, pred[9216]{0:T(1024)(128)(4,1)S(1)} %broadcast_in_dim.143), kind=kOutput, calls=%fused_computation.21.clone.1 | convolution fusion | flops 632324096 | bytes 21312516 | tf_op jit(solution)/shard_map/while/body/eval_jaxpr/dot_general | solution.py:51
  118.3 11.7 %fusion.106 = f32[512]{0:T(512)S(1)} fusion(f32[512,9216]{1,0:T(8,128)} %get-tuple-element.264, f32[512]{0:T(512)S(1)} %get-tuple-element.265, f32[]{:T(128)} %get-tuple-element.293, pred[9216]{0:T(1024)(128)(4,1)S(1)} %broadcast_in_dim.143), kind=kLoop, calls=%fused_computation.10.clone.1 | loop fusion | flops 23592448 | bytes 18887684 | tf_op jit(solution)/shard_map/while/body/eval_jaxpr/reduce_sum | solution.py:49
  130.0 11.1 %fusion.107 = bf16[1,512,64]{1,2,0:T(8,128)(2,1)S(1)} fusion(bf16[9216,128]{1,0:T(8,128)(2,1)} %get-tuple-element.292, f32[512,9216]{1,0:T(8,128)} %get-tuple-element.264, f32[512]{0:T(512)S(1)} %fusion.106, f32[512]{0:T(512)S(1)} %get-tuple-element.265, f32[]{:T(128)} %get-tuple-element.293, pred[9216]{0:T(1024)(128)(4,1)S(1)} %broadcast_in_dim.143), kind=kOutput, calls=%fused_computation.22.clone.1 | convolution fusion | flops 632324096 | bytes 21312516 | tf_op jit(solution)/shard_map/while/body/eval_jaxpr/dot_general | solution.py:51
  142.1 7.8 %fusion.104 = (f32[512]{0:T(512)S(1)}, f32[512,9216]{1,0:T(8,128)}) fusion(f32[]{:T(128)} %get-tuple-element.291, pred[9216]{0:T(1024)(128)(4,1)S(1)} %broadcast_in_dim.143, bf16[9216,128]{1,0:T(8,128)(2,1)S(1)} %get-tuple-element.290, bf16[512,128]{1,0:T(8,128)(2,1)S(1)} %dynamic-slice_bitcast_fusion.2), kind=kOutput, calls=%fused_computation.7.clone.1 | convolution fusion | flops 618135040 | bytes 21376004 | tf_op jit(solution)/shard_map/while/body/eval_jaxpr/dot_general | solution.py:37
  149.9 18.1 %fusion.105 = (f32[512]{0:T(512)S(1)}, f32[512]{0:T(512)S(1)}, f32[512,9216]{1,0:T(8,128)}) fusion(f32[512,9216]{1,0:T(8,128)} %get-tuple-element.262, f32[512]{0:T(512)S(1)} %get-tuple-element.263, f32[]{:T(128)} %get-tuple-element.291, pred[9216]{0:T(1024)(128)(4,1)S(1)} %broadcast_in_dim.143, f32[]{:T(128)} %get-tuple-element.293, ...), kind=kOutput, calls=%fused_computation.9.clone.1 | convolution fusion | flops 641727488 | bytes 40254472 | tf_op jit(solution)/shard_map/while/body/eval_jaxpr/dot_general | solution.py:37
  168.1 9.4 %fusion.108 = bf16[1,512,64]{1,2,0:T(8,128)(2,1)S(1)} fusion(bf16[9216,128]{1,0:T(8,128)(2,1)S(1)} %copy-done.4, f32[512,9216]{1,0:T(8,128)} %get-tuple-element.262, f32[512]{0:T(512)S(1)} %get-tuple-element.266, f32[512]{0:T(512)S(1)} %get-tuple-element.263, f32[]{:T(128)} %get-tuple-element.291, pred[9216]{0:T(1024)(128)(4,1)S(1)} %broadcast_in_dim.143), kind=kOutput, calls=%fused_computation.21.clone.1 | convolution fusion | flops 632324096 | bytes 21312516 | tf_op jit(solution)/shard_map/while/body/eval_jaxpr/dot_general | solution.py:51
  177.5 11.7 %fusion.106 = f32[512]{0:T(512)S(1)} fusion(f32[512,9216]{1,0:T(8,128)} %get-tuple-element.264, f32[512]{0:T(512)S(1)} %get-tuple-element.265, f32[]{:T(128)} %get-tuple-element.293, pred[9216]{0:T(1024)(128)(4,1)S(1)} %broadcast_in_dim.143), kind=kLoop, calls=%fused_computation.10.clone.1 | loop fusion | flops 23592448 | bytes 18887684 | tf_op jit(solution)/shard_map/while/body/eval_jaxpr/reduce_sum | solution.py:49
  189.2 11.1 %fusion.107 = bf16[1,512,64]{1,2,0:T(8,128)(2,1)S(1)} fusion(bf16[9216,128]{1,0:T(8,128)(2,1)} %get-tuple-element.292, f32[512,9216]{1,0:T(8,128)} %get-tuple-element.264, f32[512]{0:T(512)S(1)} %fusion.106, f32[512]{0:T(512)S(1)} %get-tuple-element.265, f32[]{:T(128)} %get-tuple-element.293, pred[9216]{0:T(1024)(128)(4,1)S(1)} %broadcast_in_dim.143), kind=kOutput, calls=%fused_computation.22.clone.1 | convolution fusion | flops 632324096 | bytes 21312516 | tf_op jit(solution)/shard_map/while/body/eval_jaxpr/dot_general | solution.py:51
  201.1 1.4 multiply_reduce_fusion
  202.5 1.2 fusion.36
  204.0 1.2 convolution_convert_fusion
  205.3 1.3 multiply_reduce_fusion.2
  206.7 57.0 %all-gather = bf16[32,4,1024]{2,1,0:T(4,128)(2,1)S(1)} all-gather(bf16[1,4,1024]{2,1,0:T(4,128)(2,1)S(1)} %fusion.59), channel_id=1, replica_groups=mesh['noise'=8,'row'=4,'col'=8] {'row','col'}, dimensions={0}, use_global_device_ids=true | all-gather | bytes 270336 | tf_op jit(solution)/shard_map/all_gather | solution.py:144
  263.8 1.5 fusion.78
  266.9 1.8 convolution_convert_fusion.1
  270.0 74.0 %all-reduce.3.cloned.1.call-done = bf16[32,1024]{1,0:T(8,128)(2,1)} async-done(((bf16[32,1024]{1,0:T(8,128)(2,1)}), bf16[32,1024]{1,0:T(8,128)(2,1)}) %all-reduce.3.cloned.1.call-update) | async-done | bytes 65552
  344.0 0.8 fusion.47
  344.9 0.8 fusion.50
  (84 shorter events, 8.4 us)
Async XLA Ops:
  7.2 41.8 %copy-start = (f32[256,1024]{1,0:T(8,128)S(1)}, f32[256,1024]{1,0:T(8,128)}, u32[]{:S(2)}) copy-start(f32[256,1024]{1,0:T(8,128)} %param.27) | copy-start | bytes 3145732
  7.2 336.8 %all-reduce.3.cloned.1.call-start = ((), (), s32[]{:S(2)}) async-start(), calls=%async_computation | async-start | bytes 131072
  12.2 2.1 copy-start.3
  12.2 30.6 %copy-start.9 = (f32[2]{0:T(128)S(1)}, f32[2]{0:T(128)}, u32[]{:S(2)}) copy-start(f32[2]{0:T(128)} %param.22) | copy-start | bytes 28
  13.4 33.6 %copy-start.10 = (f32[2]{0:T(128)S(1)}, f32[2]{0:T(128)}, u32[]{:S(2)}) copy-start(f32[2]{0:T(128)} %param.29) | copy-start | bytes 28
  25.1 3.3 collective-permute-start
  26.9 5.1 %collective-permute-start.1 = (bf16[2,32,32,128]{3,2,1,0:T(8,128)(2,1)S(1)}, bf16[2,32,32,128]{3,2,1,0:T(8,128)(2,1)S(1)}, u32[]{:S(2)}, u32[]{:S(2)}) collective-permute-start(bf16[2,32,32,128]{3,2,1,0:T(8,128)(2,1)S(1)} %pad_maximum_fusion.3), channel_id=1, source_target_pairs={{8,0},{16,8},{24,16},{9,1},{17,9},{25,17},{10,2},{18,10},{26,18},{... | collective-permute-start | bytes 1572872 | tf_op jit(solution)/shard_map/ppermute | solution.py:19
  33.3 32.2 %collective-permute-start.2 = (bf16[2,96,32,128]{3,2,1,0:T(8,128)(2,1)}, bf16[2,96,32,128]{3,2,1,0:T(8,128)(2,1)}, u32[]{:S(2)}, u32[]{:S(2)}) collective-permute-start(bf16[2,96,32,128]{3,2,1,0:T(8,128)(2,1)} %pad_maximum_fusion.2), channel_id=1, source_target_pairs={{0,1},{1,2},{2,3},{3,4},{4,5},{5,6},{6,7},{8,9},{9,10},{10,11},{11... | collective-permute-start | bytes 4718600 | tf_op jit(solution)/shard_map/ppermute | solution.py:18
  38.3 33.1 %collective-permute-start.3 = (bf16[2,96,32,128]{3,2,1,0:T(8,128)(2,1)}, bf16[2,96,32,128]{3,2,1,0:T(8,128)(2,1)}, u32[]{:S(2)}, u32[]{:S(2)}) collective-permute-start(bf16[2,96,32,128]{3,2,1,0:T(8,128)(2,1)} %pad_maximum_fusion.2), channel_id=1, source_target_pairs={{1,0},{2,1},{3,2},{4,3},{5,4},{6,5},{7,6},{9,8},{10,9},{11,10},{12... | collective-permute-start | bytes 4718600 | tf_op jit(solution)/shard_map/ppermute | solution.py:19
  50.1 32.3 %copy-start.2 = (bf16[2,512,128]{2,1,0:T(8,128)(2,1)S(1)}, bf16[2,512,128]{2,1,0:T(8,128)(2,1)}, u32[]{:S(2)}) copy-start(bf16[2,512,128]{2,1,0:T(8,128)(2,1)} %copy.39) | copy-start | bytes 786436
  82.4 118.7 %copy-start.6 = (bf16[128,128]{1,0:T(8,128)(2,1)S(1)}, bf16[128,128]{1,0:T(8,128)(2,1)}, u32[]{:S(2)}) copy-start(bf16[128,128]{1,0:T(8,128)(2,1)} %param.23) | copy-start | bytes 98308
  82.4 120.1 %copy-start.11 = (f32[128]{0:T(128)S(1)}, f32[128]{0:T(128)}, u32[]{:S(2)}) copy-start(f32[128]{0:T(128)} %param.24) | copy-start | bytes 1540
  82.4 124.2 %copy-start.7 = (f32[1024]{0:T(1024)S(1)}, f32[1024]{0:T(1024)}, u32[]{:S(2)}) copy-start(f32[1024]{0:T(1024)} %broadcast_add_fusion) | copy-start | bytes 12292
  82.4 186.3 %copy-start.12 = (u32[256]{0:T(256)S(1)}, u32[256]{0:T(256)}, u32[]{:S(2)}) copy-start(u32[256]{0:T(256)} %constant.97) | copy-start | bytes 3076
  82.5 262.4 %copy-start.8 = (f32[1024]{0:T(1024)S(1)}, f32[1024]{0:T(1024)}, u32[]{:S(2)}) copy-start(f32[1024]{0:T(1024)} %param.31) | copy-start | bytes 12292
  90.7 18.1 %copy-start.4 = (bf16[9216,128]{1,0:T(8,128)(2,1)S(1)}, bf16[9216,128]{1,0:T(8,128)(2,1)}, u32[]{:S(2)}) copy-start(bf16[9216,128]{1,0:T(8,128)(2,1)} %get-tuple-element.292) | copy-start | bytes 7077892 | tf_op jit(solution)/shard_map/while
  149.9 18.1 %copy-start.4 = (bf16[9216,128]{1,0:T(8,128)(2,1)S(1)}, bf16[9216,128]{1,0:T(8,128)(2,1)}, u32[]{:S(2)}) copy-start(bf16[9216,128]{1,0:T(8,128)(2,1)} %get-tuple-element.292) | copy-start | bytes 7077892 | tf_op jit(solution)/shard_map/while
  201.1 145.2 %copy-start.1 = (f32[256,1024]{1,0:T(8,128)S(1)}, f32[256,1024]{1,0:T(8,128)}, u32[]{:S(2)}) copy-start(f32[256,1024]{1,0:T(8,128)} %param.27) | copy-start | bytes 3145732
  203.7 142.6 %copy-start.5 = (bf16[32,32,128]{2,1,0:T(8,128)(2,1)}, bf16[32,32,128]{2,1,0:T(8,128)(2,1)S(1)}, u32[]{:S(2)}) copy-start(bf16[32,32,128]{2,1,0:T(8,128)(2,1)S(1)} %fusion.36) | copy-start | bytes 786436
Sparse Core Ops, SparseCore 0:
  268.9 75.0 all-reduce.2
where the time goes:
time: 354 us; the launch traced here: 353 us
  matrix products  106 us (30%)
  waiting for transfers between devices  99.1 us (28%)
  blocking collectives  57 us (16%)
  other arithmetic  44.3 us (13%)
  local copies, waits for them, and re-layouts  18.8 us (5%)
  between operations  18.3 us (5%)
  starting transfers between devices  9.34 us (3%)
    unnamed x2, waiting for transfers between devices  74 us
    all_gather x1, blocking collectives, body(): lax.all_gather(cn, ('row', 'col'), axis=0, tiled=True)  57 us
    dot_general x6, matrix products, attend(): jnp.dot(queries[:, low:low + HEAD], keys[:, low:low + HEAD].T, preferred_...  52.5 us
    dot_general x6, matrix products, attend(): jnp.dot(weights, values[:, low:low + HEAD], preferred_element_type=jnp.fl...  41.3 us
    reduce_sum x4, other arithmetic, attend(): jnp.sum(expo, axis=-1, keepdims=True)  23.8 us
    ppermute x2, waiting for transfers between devices, with_halo(): before = lax.ppermute(last, axis, up)  15.6 us
    concatenate x2, other arithmetic, with_halo(): x = jnp.concatenate([before, x, after], axis=dim)  10.2 us
    ppermute x2, waiting for transfers between devices, with_halo(): after = lax.ppermute(initial, axis, down)  9.45 us
  transfers between devices with their start and end apart: 5, of which 5 were waited for; matrix products, arithmetic and copies ran while one was open for 2% of the time, Pallas kernels for 0%

commit v1 on v0

v1 whole, which is shorter than its diff:
```python
import functools

import jax
import jax.numpy as jnp
from jax import lax
from jax.experimental import pallas as pl
from jax.experimental.pallas import tpu as pltpu
from jax.sharding import PartitionSpec as P

HEAD = 64
POOL = 8
EPS = 1e-06
LOG2E = 1.4426950408889634
QCHUNK = 256
VMEM_LIMIT = 40 * 1024 * 1024
NT = (((1,), (1,)), ((), ()))
NN = (((1,), (0,)), ((), ()))
F32 = jnp.float32
BF16 = jnp.bfloat16


def mm(a, b, dims=NN):
    return lax.dot_general(a, b, dims, preferred_element_type=F32)


def rms_rows(value):
    return value * lax.rsqrt(jnp.mean(value * value, axis=-1, keepdims=True) + EPS)


def head_means(value):
    width = value.shape[1]
    i = lax.broadcasted_iota(jnp.int32, (width, width), 0) // HEAD
    j = lax.broadcasted_iota(jnp.int32, (width, width), 1) // HEAD
    ones = jnp.where(i == j, 1.0 / HEAD, 0.0).astype(BF16)
    return mm((value * value).astype(BF16), ones)


def low_lanes(shape):
    return lax.broadcasted_iota(jnp.int32, shape, 1) < HEAD


def level_row(level_ref, table_ref):
    table = table_ref[...]
    ids = lax.broadcasted_iota(jnp.int32, table.shape, 0)
    return jnp.sum(jnp.where(ids == level_ref[0], table, 0.0), axis=0, keepdims=True)


def gain_row(cond, ada_ref):
    return 1.0 + lax.dot_general(
        cond, ada_ref[...], NN, precision=lax.Precision.HIGHEST, preferred_element_type=F32
    )


def tile_kv(x, gain, wkv, valid):
    width = x.shape[1]
    xn = (rms_rows(x.astype(F32)) * gain).astype(BF16)
    proj = mm(xn, wkv)
    k = proj[:, :width]
    k = (k * lax.rsqrt(head_means(k) + EPS)).astype(BF16)
    v = proj[:, width:]
    low = low_lanes(v.shape)
    v0 = jnp.where(low, v, valid).astype(BF16)
    v1 = jnp.where(low, valid, v).astype(BF16)
    return xn, k, v0, v1


def attend_tile(q_refs, k, vs, acc_refs, first):
    for start in range(0, q_refs[0].shape[0], QCHUNK):
        rows = pl.ds(start, QCHUNK)
        for q_ref, v, acc_ref in zip(q_refs, vs, acc_refs):
            p = jnp.exp2(mm(q_ref[rows, :], k, NT)).astype(BF16)
            part = mm(p, v)
            if first:
                acc_ref[rows, :] = part
            else:
                acc_ref[rows, :] += part


def own_kernel(level, scale, x, table, ada, wqkv, q0, q1, acc0, acc1, gain_out):
    width = x.shape[1]
    gain = gain_row(level_row(level, table), ada)
    gain_out[...] = gain
    xn, k, v0, v1 = tile_kv(x[...], gain, wqkv[:, width:], 1.0)
    q = mm(xn, wqkv[:, :width])
    low = low_lanes(q.shape)
    factor = jnp.where(low, scale[0], scale[1]) * (LOG2E / HEAD)
    q = q * lax.rsqrt(head_means(q) + EPS) * factor
    q0[...] = jnp.where(low, q, 0.0).astype(BF16)
    q1[...] = jnp.where(low, 0.0, q).astype(BF16)
    attend_tile((q0, q1), k, (v0, v1), (acc0, acc1), True)


def edge_flags():
    row, col = lax.axis_index("row"), lax.axis_index("col")
    row_ok = (row > 0) & (row < lax.axis_size("row") - 1)
    col_ok = (col > 0) & (col < lax.axis_size("col") - 1)
    return jnp.where(row_ok, 1.0, 0.0), jnp.where(col_ok, 1.0, 0.0)


def more_tiles(which, tiles, gain, wqkv, q_refs, acc_refs):
    width = wqkv.shape[0]
    row_ok, col_ok = edge_flags()
    flags = {"col": (1.0, col_ok), "near": (1.0, 1.0, col_ok), "far": (row_ok, row_ok, row_ok * col_ok)}
    for at, valid in enumerate(flags[which]):
        _, k, v0, v1 = tile_kv(tiles[at][...], gain[...], wqkv[:, width:], valid)
        attend_tile(q_refs, k, (v0, v1), acc_refs, False)


def col_kernel(a, b, gain, wqkv, q0, q1, acc0_in, acc1_in, acc0, acc1):
    acc0[...] = acc0_in[...]
    acc1[...] = acc1_in[...]
    more_tiles("col", (a, b), gain, wqkv, (q0, q1), (acc0, acc1))


def near_kernel(tiles, gain, wqkv, q0, q1, acc0_in, acc1_in, acc0, acc1):
    acc0[...] = acc0_in[...]
    acc1[...] = acc1_in[...]
    more_tiles("near", [tiles.at[i] for i in range(3)], gain, wqkv, (q0, q1), (acc0, acc1))


def far_kernel(
    tiles, gain, wqkv, q0, q1, acc0_in, acc1_in, x, wout, post, wmerge, out, pooled, acc0, acc1
):
    acc0[...] = acc0_in[...]
    acc1[...] = acc1_in[...]
    more_tiles("far", [tiles.at[i] for i in range(3)], gain, wqkv, (q0, q1), (acc0, acc1))
    tokens, width = x.shape
    low = low_lanes((tokens, width))
    a0, a1 = acc0[...], acc1[...]
    sums = pltpu.roll(jnp.where(low, a1, a0), HEAD, 1)
    attended = (jnp.where(low, a0, a1) / sums).astype(BF16)
    branch = mm(attended, wout[...])
    result = (x[...].astype(F32) + rms_rows(branch) * post[...]).astype(BF16)
    out[...] = result
    side = 32
    group = lax.broadcasted_iota(jnp.int32, (16, tokens), 0)
    token = lax.broadcasted_iota(jnp.int32, (16, tokens), 1)
    i, j = token // side, token % side
    place = ((i % 2) * 2 + j % 2) * 4 + (i // (2 * POOL)) * 2 + j // (2 * POOL)
    pick = jnp.where(group == place, 1.0 / (POOL * POOL), 0.0).astype(BF16)
    means = mm(pick, result)
    high = means.astype(BF16)
    rest = (means - high.astype(F32)).astype(BF16)
    total = jnp.zeros((4, wmerge.shape[1]), F32)
    for part in range(4):
        w = wmerge[pl.ds(part * width, width), :]
        at = slice(4 * part, 4 * part + 4)
        total += mm(high[at], w) + mm(rest[at], w)
    pooled[...] = jnp.broadcast_to(total.astype(BF16)[None], pooled.shape)


def coarse_kernel(
    level, scale, tokens, table, ada, win, wqkv, wout, own, part_out, coarse_in_out, cn_ref, in_ref
):
    row, col = lax.axis_index("row"), lax.axis_index("col")
    count = tokens.shape[0]
    rows_each = count // lax.axis_size("row")
    own_each = rows_each // lax.axis_size("col")
    gain = gain_row(level_row(level, table), ada)
    coarse_in = mm(tokens[...], win[...])
    coarse_in_out[...] = mm(own[...], win[...])
    cn = (rms_rows(coarse_in) * gain).astype(BF16)
    cn_ref[...] = (rms_rows(coarse_in) * gain)
    mine = cn_ref[pl.ds(pl.multiple_of(row * rows_each, rows_each), rows_each), :].astype(BF16)
    q, k, v = mm(mine, wqkv[0]), mm(cn, wqkv[1]), mm(cn, wqkv[2])
    low = low_lanes(q.shape)
    factor = jnp.where(low, scale[0], scale[1]) * (LOG2E / HEAD)
    q = q * lax.rsqrt(head_means(q) + EPS) * factor
    k = (k * lax.rsqrt(head_means(k) + EPS)).astype(BF16)
    wide = low_lanes(v.shape)
    v0 = jnp.where(wide, v, 1.0).astype(BF16)
    v1 = jnp.where(wide, 1.0, v).astype(BF16)
    q0 = jnp.where(low, q, 0.0).astype(BF16)
    q1 = jnp.where(low, 0.0, q).astype(BF16)
    a0 = mm(jnp.exp2(mm(q0, k, NT)).astype(BF16), v0)
    a1 = mm(jnp.exp2(mm(q1, k, NT)).astype(BF16), v1)
    sums = pltpu.roll(jnp.where(low, a1, a0), HEAD, 1)
    attended = (jnp.where(low, a0, a1) / sums).astype(BF16)
    part_out[...] = mm(attended, wout[...]).astype(BF16).reshape(part_out.shape)


def final_kernel(parts, coarse_in, post, out):
    branch = jnp.sum(parts[...].astype(F32), axis=0)
    out[...] = (coarse_in[...] + rms_rows(branch) * post[...]).astype(BF16)


def call(kernel, out_shape, args, smem=0, scratch=(), aliases=None, flops=0, name=None):
    vmem = pl.BlockSpec(memory_space=pltpu.VMEM)
    scalars = pl.BlockSpec(memory_space=pltpu.SMEM)
    moved = sum(a.size * a.dtype.itemsize for a in args)
    return pl.pallas_call(
        kernel,
        out_shape=out_shape,
        in_specs=[scalars] * smem + [vmem] * (len(args) - smem),
        out_specs=jax.tree.map(lambda _: vmem, out_shape),
        scratch_shapes=list(scratch),
        input_output_aliases=aliases or {},
        compiler_params=pltpu.CompilerParams(vmem_limit_bytes=VMEM_LIMIT),
        cost_estimate=pl.CostEstimate(flops=flops, bytes_accessed=moved, transcendentals=0),
        name=name,
    )(*args)


def body(
    image,
    noise_level,
    cond_table,
    ada_fine,
    fine_qkv,
    fine_scale,
    fine_out_w,
    fine_post,
    merge_w,
    coarse_in_w,
    ada_coarse,
    coarse_qkv,
    coarse_scale,
    coarse_out_w,
    coarse_post,
):
    shape = jax.ShapeDtypeStruct
    rows, cols, width = image.shape
    count = rows * cols
    n_row, n_col = lax.axis_size("row"), lax.axis_size("col")
    x = image.reshape(count, width)

    def swaps(n, odd):
        pairs = [(i, i + 1) for i in range(odd, n - 1, 2)]
        return pairs + [(j, i) for i, j in pairs]

    tile_flops = 4 * count * count * width * 4
    col_a = lax.ppermute(x, "col", swaps(n_col, 0))
    col_b = lax.ppermute(x, "col", swaps(n_col, 1))
    q0, q1, acc0, acc1, gain = call(
        own_kernel,
        (shape((count, width), BF16),) * 2 + (shape((count, width), F32),) * 2 + (shape((1, width), F32),),
        (noise_level, fine_scale, x, cond_table, ada_fine, fine_qkv),
        smem=2,
        flops=tile_flops,
        name="own_tile",
    )
    held, gain = lax.optimization_barrier((x, gain))
    three = jnp.stack([held, col_a, col_b])
    near = lax.ppermute(three, "row", swaps(n_row, 0))
    far = lax.ppermute(three, "row", swaps(n_row, 1))
    accs = (shape((count, width), F32),) * 2
    acc0, acc1 = call(
        col_kernel,
        accs,
        (col_a, col_b, gain, fine_qkv, q0, q1, acc0, acc1),
        flops=2 * tile_flops,
        name="col_tiles",
    )
    acc0, acc1 = call(
        near_kernel,
        accs,
        (near, gain, fine_qkv, q0, q1, acc0, acc1),
        flops=3 * tile_flops,
        name="near_row_tiles",
    )
    devices = n_row * n_col
    merge_width = merge_w.shape[1]
    fine_out, pooled = call(
        far_kernel,
        (shape((count, width), BF16), shape((devices, 4, merge_width), BF16)),
        (far, gain, fine_qkv, q0, q1, acc0, acc1, x, fine_out_w, fine_post[None], merge_w),
        scratch=[pltpu.VMEM((count, width), F32)] * 2,
        flops=3 * tile_flops,
        name="far_row_tiles",
    )
    tokens = lax.all_to_all(pooled, ("row", "col"), 0, 0, tiled=True)
    coarse_width = coarse_in_w.shape[1]
    own = 4
    parts, coarse_in = call(
        coarse_kernel,
        (shape((n_col, own, coarse_width), BF16), shape((own, coarse_width), F32)),
        (
            noise_level,
            coarse_scale,
            tokens.reshape(-1, merge_width),
            cond_table,
            ada_coarse,
            coarse_in_w,
            coarse_qkv,
            coarse_out_w,
            pooled[0],
        ),
        smem=2,
        scratch=[pltpu.VMEM((devices * own, coarse_width), F32)] * 2,
        name="coarse",
    )
    parts = lax.all_to_all(parts, "col", 0, 0, tiled=True)
    coarse_out = call(
        final_kernel,
        shape((own, coarse_width), BF16),
        (parts, coarse_in, coarse_post[None]),
        name="coarse_out",
    )
    pooled_rows, pooled_cols = rows // (2 * POOL), cols // (2 * POOL)
    return fine_out.reshape(rows, cols, width), coarse_out.reshape(pooled_rows, pooled_cols, coarse_width)


def solution(mesh):
    in_specs = (
        P(("noise", "row"), "col", None),
        P("noise"),
        P(),
        P(),
        P(),
        P(),
        P(),
        P(),
        P(),
        P(),
        P(),
        P(None, None, "col"),
        P("col"),
        P("col", None),
        P(),
    )
    out_specs = (P(("noise", "row"), "col", None), P(("noise", "row"), "col", None))
    return jax.shard_map(body, mesh=mesh, in_specs=in_specs, out_specs=out_specs, check_vma=False)
```

time: 354 us -> 72.6 us (0.21)
  matrix products: 106 us -> 0 us
  waiting for transfers between devices: 99.1 us -> 8.08 us
  blocking collectives: 57 us -> 10.9 us
  other arithmetic: 44.3 us -> 0.09 us
  Pallas kernels: 0 us -> 29.4 us
  between operations: 18.3 us -> 1.55 us
  local copies, waits for them, and re-layouts: 18.8 us -> 5.43 us
  starting transfers between devices: 9.34 us -> 16.8 us
    dot_general x21 -> x0, matrix products: 104 us -> none  [the longest x6 52.5 us: attend(): jnp.dot(queries[:, low:low + HEAD], keys[:, low:low + HEAD].T, preferred_...]
    unnamed x2 -> x0, waiting for transfers between devices: 74 us -> none
    all_gather x1 -> x0, blocking collectives: 57 us -> none  [body(): lax.all_gather(cn, ('row', 'col'), axis=0, tiled=True)]
    pallas_call x0 -> x6, Pallas kernels: none -> 29.4 us  [call(): pl.pallas_call(kernel, out_shape=out_shape, in_specs=[scalars] * smem + [...]
    reduce_sum x10 -> x0, other arithmetic: 27.9 us -> none  [the longest x4 23.8 us: attend(): jnp.sum(expo, axis=-1, keepdims=True)]
    ppermute x4, waiting for transfers between devices: 25.1 us -> 0.01 us  [the longest x1 0.01 us: body(): col_a = lax.ppermute(x, 'col', swaps(n_col, 0))]
    all_to_all x0 -> x1, blocking collectives: none -> 10.9 us  [body(): parts = lax.all_to_all(parts, 'col', 0, 0, tiled=True)]
    concatenate x4 -> x0, other arithmetic: 10.2 us -> none  [the longest x2 10.2 us: with_halo(): x = jnp.concatenate([before, x, after], axis=dim)]
  transfers between devices with their start and end apart: 5 -> 5, of which waited for: 5 -> 1; matrix products, arithmetic and copies ran while one was open for 2% -> 1% of each run, Pallas kernels for 0% -> 24%
where the time goes in v1:
time: 72.6 us; the launch traced here: 72.2 us
  Pallas kernels  29.4 us (40%)
  starting transfers between devices  16.8 us (23%)
  blocking collectives  10.9 us (15%)
  waiting for transfers between devices  8.08 us (11%)
  local copies, waits for them, and re-layouts  5.43 us (7%)
  between operations  1.55 us (2%)
    pallas_call x6, Pallas kernels, call(): pl.pallas_call(kernel, out_shape=out_shape, in_specs=[scalars] * smem + [...  29.4 us
    all_to_all x1, blocking collectives, body(): parts = lax.all_to_all(parts, 'col', 0, 0, tiled=True)  10.9 us
    all_to_all x1, starting transfers between devices, body(): tokens = lax.all_to_all(pooled, ('row', 'col'), 0, 0, tiled=True)  9.94 us
    all_to_all x1, waiting for transfers between devices, body(): tokens = lax.all_to_all(pooled, ('row', 'col'), 0, 0, tiled=True)  8.07 us
    ppermute x1, starting transfers between devices, body(): col_a = lax.ppermute(x, 'col', swaps(n_col, 0))  5.15 us
    unnamed x34, local copies, waits for them, and re-layouts  4.12 us
  transfers between devices with their start and end apart: 5, of which 1 were waited for; matrix products, arithmetic and copies ran while one was open for 1% of the time, Pallas kernels for 24%

profile of v1, /device:TPU:2, one launch (start us, length us, event | category | flops | bytes accessed | tf_op | source)
XLA Modules:
  0.0 72.2 jit_solution(17610594896641161725)
XLA Ops:
  0.6 0.0 copy-start.15
  0.6 0.7 collective-permute-start.1
  1.3 5.2 %collective-permute-start = (bf16[1024,128]{1,0:T(8,128)(2,1)}, bf16[1024,128]{1,0:T(8,128)(2,1)S(1)}, u32[]{:S(2)}, u32[]{:S(2)}) collective-permute-start(bf16[1024,128]{1,0:T(8,128)(2,1)} %bitcast.10), channel_id=1, source_target_pairs={{0,1},{2,3},{4,5},{6,7},{1,0},{3,2},{5,4},{7,6},{8,9},{10,11},{12,... | collective-permute-start | bytes 786440 | tf_op jit(solution)/shard_map/ppermute | solution.py:232
  7.1 0.0 copy-done.15
  7.1 0.0 copy-start.3
  7.2 0.9 %copy-done.3 = bf16[32,32,128]{2,1,0:T(8,128)(2,1)S(1)} copy-done((bf16[32,32,128]{2,1,0:T(8,128)(2,1)S(1)}, bf16[32,32,128]{2,1,0:T(8,128)(2,1)}, u32[]{:S(2)}) %copy-start.3) | copy-done | bytes 262168
  8.1 0.0 copy-start.6
  8.1 0.7 copy-done.6
  8.8 0.9 %copy-done.11 = f32[256,128]{1,0:T(8,128)S(1)} copy-done((f32[256,128]{1,0:T(8,128)S(1)}, f32[256,128]{1,0:T(8,128)}, u32[]{:S(2)}) %copy-start.11) | copy-done | bytes 131096
  9.7 0.0 copy-start.12
  9.7 0.9 %copy-done.12 = bf16[128,384]{1,0:T(8,128)(2,1)S(1)} copy-done((bf16[128,384]{1,0:T(8,128)(2,1)S(1)}, bf16[128,384]{1,0:T(8,128)(2,1)}, u32[]{:S(2)}) %copy-start.12) | copy-done | bytes 98328
  10.6 3.8 %own_tile.1 = (bf16[1024,128]{1,0:T(8,128)(2,1)S(1)}, bf16[1024,128]{1,0:T(8,128)(2,1)S(1)}, f32[1024,128]{1,0:T(8,128)S(1)}, f32[1024,128]{1,0:T(8,128)S(1)}, f32[1,128]{1,0:T(1,128)S(1)}) custom-call(s32[1]{0:T(128)S(6)} %copy.17.level, f32[2]{0:T(128)S(1)} %copy-done.15, bf16[1024,128]{1,0:T(8,128)(2,1)S(1)} %bitcast.11, f32[8,256]{1,0:T(8,128)S(1)} %copy-done.6, ...), custom_call_target="tpu_custom_call" | custom-call | flops 2147483648 | bytes 499724 | tf_op jit(solution)/shard_map/own_tile/pallas_call | solution.py:191
  14.4 0.0 collective-permute-done.1.b
  14.4 0.0 collective-permute-done.a
  14.4 0.0 copy-start.13
  14.4 0.1 pad_maximum_fusion
  14.5 0.1 collective-permute-start.3
  14.6 0.9 %collective-permute-start.2 = (bf16[3,1024,128]{2,1,0:T(8,128)(2,1)S(1)}, bf16[3,1024,128]{2,1,0:T(8,128)(2,1)S(1)}, u32[]{:S(2)}, u32[]{:S(2)}) collective-permute-start(bf16[3,1024,128]{2,1,0:T(8,128)(2,1)S(1)} %pad_maximum_fusion), channel_id=1, source_target_pairs={{8,16},{16,8},{9,17},{17,9},{10,18},{18,10},{11,19},{19,11},{12,20... | collective-permute-start | bytes 2359304 | tf_op jit(solution)/shard_map/ppermute | solution.py:245
  15.5 0.0 copy-done.13
  15.5 5.5 %col_tiles.1 = (f32[1024,128]{1,0:T(8,128)S(1)}, f32[1024,128]{1,0:T(8,128)S(1)}) custom-call(bf16[1024,128]{1,0:T(8,128)(2,1)S(1)} %collective-permute-done.a, bf16[1024,128]{1,0:T(8,128)(2,1)S(1)} %collective-permute-done.1.b, f32[1,128]{1,0:T(1,128)S(1)} %get-tuple-element.19.gain, bf16[128,384]{1,0:T(8,128)(2,1)S(1)} %copy-done.13, ...), custom_call_target="tpu_custom_call" | custom-call | flops 4294967296 | bytes 2195968 | tf_op jit(solution)/shard_map/col_tiles/pallas_call | solution.py:191
  21.0 0.0 collective-permute-done.3.tiles
  21.0 0.0 copy-start.4
  21.0 0.0 copy-start.10
  21.0 0.0 copy-start.14
  21.0 8.3 %near_row_tiles.1 = (f32[1024,128]{1,0:T(8,128)S(1)}, f32[1024,128]{1,0:T(8,128)S(1)}) custom-call(bf16[3,1024,128]{2,1,0:T(8,128)(2,1)S(1)} %collective-permute-done.3.tiles, f32[1,128]{1,0:T(1,128)S(1)} %get-tuple-element.19.gain, bf16[128,384]{1,0:T(8,128)(2,1)S(1)} %copy-done.13, bf16[1024,128]{1,0:T(8,128)(2,1)S(1)} %get-tuple-element.20.q0, ...), custom_call_target="tpu_custom_call" | custom-call | flops 6442450944 | bytes 2458112 | tf_op jit(solution)/shard_map/near_row_tiles/pallas_call | solution.py:191
  29.3 0.0 collective-permute-done.2.tiles
  29.3 0.0 copy-start.16
  29.3 0.0 copy-done.4
  29.3 0.0 copy-done.10
  29.3 0.0 copy-done.14
  29.4 0.6 copy-done.16
  30.0 0.0 copy-start
  30.0 9.4 %far_row_tiles.1 = (bf16[1024,128]{1,0:T(8,128)(2,1)}, bf16[32,4,256]{2,1,0:T(4,128)(2,1)}) custom-call(bf16[3,1024,128]{2,1,0:T(8,128)(2,1)S(1)} %collective-permute-done.2.tiles, f32[1,128]{1,0:T(1,128)S(1)} %get-tuple-element.19.gain, bf16[128,384]{1,0:T(8,128)(2,1)S(1)} %copy-done.13, bf16[1024,128]{1,0:T(8,128)(2,1)S(1)} %get-tuple-element.20.q0, ...), custom_call_target="tpu_custom_call" | custom-call | flops 6442450944 | bytes 3015680 | tf_op jit(solution)/shard_map/far_row_tiles/pallas_call | solution.py:191
  39.4 9.9 %all-to-all-start = ((bf16[32,4,256]{2,1,0:T(4,128)(2,1)}), bf16[32,4,256]{2,1,0:T(4,128)(2,1)S(1)}, u32[]{:S(2)}, u32[]{:S(2)}) async-start(bf16[32,4,256]{2,1,0:T(4,128)(2,1)} %get-tuple-element.29), calls=%async_computation | async-start | bytes 131072 | tf_op jit(solution)/shard_map/all_to_all | solution.py:271
  49.3 0.7 slice_bitcast_fusion.own
  50.0 8.1 %all-to-all-done = bf16[32,4,256]{2,1,0:T(4,128)(2,1)S(1)} async-done(((bf16[32,4,256]{2,1,0:T(4,128)(2,1)}), bf16[32,4,256]{2,1,0:T(4,128)(2,1)S(1)}, u32[]{:S(2)}, u32[]{:S(2)}) %all-to-all-start) | async-done | bytes 65568 | tf_op jit(solution)/shard_map/all_to_all | solution.py:271
  58.1 0.0 copy-done
  58.1 0.0 copy-done.1
  58.1 0.0 copy-done.2
  58.1 0.0 copy-done.7
  58.1 0.0 copy-done.5
  58.1 0.0 copy-done.9
  58.2 2.3 %coarse.1 = (bf16[8,4,1024]{2,1,0:T(4,128)(2,1)S(1)}, f32[4,1024]{1,0:T(4,128)S(1)}) custom-call(s32[1]{0:T(128)S(6)} %copy.17.level, f32[2]{0:T(128)S(1)} %copy-done.9, bf16[128,256]{1,0:T(8,128)(2,1)S(1)} %reshape.18.tokens, f32[8,256]{1,0:T(8,128)S(1)} %copy-done.7, f32[256,1024]{1,0:T(8,128)S(1)} %copy-done, bf16[256,1024]{1,0:T(8,128)(2,1)S(1)} %copy-done.2, ...), custom_call_target="tpu_custom_call" | custom-call | bytes 2697228 | tf_op jit(solution)/shard_map/coarse/pallas_call | solution.py:191
  60.5 0.0 copy-start.8
  60.5 10.9 %all_to_all.10.parts = bf16[8,4,1024]{2,1,0:T(4,128)(2,1)S(1)} all-to-all(bf16[8,4,1024]{2,1,0:T(4,128)(2,1)S(1)} %get-tuple-element.30), channel_id=1, replica_groups=mesh['noise'=8,'row'=4,'col'=8] {'col'}, dimensions={0} | all-to-all | bytes 131072 | tf_op jit(solution)/shard_map/all_to_all | solution.py:292
  71.4 0.0 copy-done.8
  71.4 0.1 coarse_out.1
  71.5 0.6 reshape.19
  (7 shorter events, 0.0 us)
Async XLA Ops:
  0.6 6.5 %copy-start.15 = (f32[2]{0:T(128)S(1)}, f32[2]{0:T(128)}, u32[]{:S(2)}) copy-start(f32[2]{0:T(128)} %scale.2) | copy-start | bytes 28
  0.6 13.7 %collective-permute-start.1 = (bf16[1024,128]{1,0:T(8,128)(2,1)}, bf16[1024,128]{1,0:T(8,128)(2,1)S(1)}, u32[]{:S(2)}, u32[]{:S(2)}) collective-permute-start(bf16[1024,128]{1,0:T(8,128)(2,1)} %bitcast.9), channel_id=1, source_target_pairs={{1,2},{3,4},{5,6},{2,1},{4,3},{6,5},{9,10},{11,12},{13,14},{10,9},... | collective-permute-start | bytes 786440 | tf_op jit(solution)/shard_map/ppermute | solution.py:233
  1.3 13.0 %collective-permute-start = (bf16[1024,128]{1,0:T(8,128)(2,1)}, bf16[1024,128]{1,0:T(8,128)(2,1)S(1)}, u32[]{:S(2)}, u32[]{:S(2)}) collective-permute-start(bf16[1024,128]{1,0:T(8,128)(2,1)} %bitcast.10), channel_id=1, source_target_pairs={{0,1},{2,3},{4,5},{6,7},{1,0},{3,2},{5,4},{7,6},{8,9},{10,11},{12,... | collective-permute-start | bytes 786440 | tf_op jit(solution)/shard_map/ppermute | solution.py:232
  7.1 1.0 %copy-start.3 = (bf16[32,32,128]{2,1,0:T(8,128)(2,1)S(1)}, bf16[32,32,128]{2,1,0:T(8,128)(2,1)}, u32[]{:S(2)}) copy-start(bf16[32,32,128]{2,1,0:T(8,128)(2,1)} %param.15) | copy-start | bytes 786436
  8.1 0.7 copy-start.6
  8.8 0.9 %copy-start.11 = (f32[256,128]{1,0:T(8,128)S(1)}, f32[256,128]{1,0:T(8,128)}, u32[]{:S(2)}) copy-start(f32[256,128]{1,0:T(8,128)} %ada.2) | copy-start | bytes 393220
  9.7 0.9 %copy-start.12 = (bf16[128,384]{1,0:T(8,128)(2,1)S(1)}, bf16[128,384]{1,0:T(8,128)(2,1)}, u32[]{:S(2)}) copy-start(bf16[128,384]{1,0:T(8,128)(2,1)} %wqkv.8) | copy-start | bytes 294916
  14.4 1.1 %copy-start.13 = (bf16[128,384]{1,0:T(8,128)(2,1)S(1)}, bf16[128,384]{1,0:T(8,128)(2,1)}, u32[]{:S(2)}) copy-start(bf16[128,384]{1,0:T(8,128)(2,1)} %wqkv.8) | copy-start | bytes 294916
  14.5 6.5 %collective-permute-start.3 = (bf16[3,1024,128]{2,1,0:T(8,128)(2,1)S(1)}, bf16[3,1024,128]{2,1,0:T(8,128)(2,1)S(1)}, u32[]{:S(2)}, u32[]{:S(2)}) collective-permute-start(bf16[3,1024,128]{2,1,0:T(8,128)(2,1)S(1)} %pad_maximum_fusion), channel_id=1, source_target_pairs={{0,8},{16,24},{8,0},{24,16},{1,9},{17,25},{9,1},{25,17},{2,10},{18... | collective-permute-start | bytes 2359304 | tf_op jit(solution)/shard_map/ppermute | solution.py:244
  14.6 14.7 %collective-permute-start.2 = (bf16[3,1024,128]{2,1,0:T(8,128)(2,1)S(1)}, bf16[3,1024,128]{2,1,0:T(8,128)(2,1)S(1)}, u32[]{:S(2)}, u32[]{:S(2)}) collective-permute-start(bf16[3,1024,128]{2,1,0:T(8,128)(2,1)S(1)} %pad_maximum_fusion), channel_id=1, source_target_pairs={{8,16},{16,8},{9,17},{17,9},{10,18},{18,10},{11,19},{19,11},{12,20... | collective-permute-start | bytes 2359304 | tf_op jit(solution)/shard_map/ppermute | solution.py:245
  21.0 8.4 %copy-start.4 = (bf16[32,32,128]{2,1,0:T(8,128)(2,1)S(1)}, bf16[32,32,128]{2,1,0:T(8,128)(2,1)}, u32[]{:S(2)}) copy-start(bf16[32,32,128]{2,1,0:T(8,128)(2,1)} %param.15) | copy-start | bytes 786436
  21.0 8.4 %copy-start.10 = (bf16[512,256]{1,0:T(8,128)(2,1)S(1)}, bf16[512,256]{1,0:T(8,128)(2,1)}, u32[]{:S(2)}) copy-start(bf16[512,256]{1,0:T(8,128)(2,1)} %wmerge.1) | copy-start | bytes 786436
  21.0 8.4 %copy-start.14 = (bf16[128,128]{1,0:T(8,128)(2,1)S(1)}, bf16[128,128]{1,0:T(8,128)(2,1)}, u32[]{:S(2)}) copy-start(bf16[128,128]{1,0:T(8,128)(2,1)} %wout.2) | copy-start | bytes 98308
  29.3 0.7 copy-start.16
  30.0 28.1 %copy-start = (f32[256,1024]{1,0:T(8,128)S(1)}, f32[256,1024]{1,0:T(8,128)}, u32[]{:S(2)}) copy-start(f32[256,1024]{1,0:T(8,128)} %ada.3) | copy-start | bytes 3145732
  30.0 28.1 %copy-start.1 = (bf16[3,1024,128]{2,1,0:T(8,128)(2,1)S(1)}, bf16[3,1024,128]{2,1,0:T(8,128)(2,1)}, u32[]{:S(2)}) copy-start(bf16[3,1024,128]{2,1,0:T(8,128)(2,1)} %wqkv.9) | copy-start | bytes 2359300
  30.0 28.1 %copy-start.2 = (bf16[256,1024]{1,0:T(8,128)(2,1)S(1)}, bf16[256,1024]{1,0:T(8,128)(2,1)}, u32[]{:S(2)}) copy-start(bf16[256,1024]{1,0:T(8,128)(2,1)} %win.1) | copy-start | bytes 1572868
  30.0 28.1 %copy-start.7 = (f32[8,256]{1,0:T(8,128)S(1)}, f32[8,256]{1,0:T(8,128)}, u32[]{:S(2)}) copy-start(f32[8,256]{1,0:T(8,128)} %table.3) | copy-start | bytes 24580
  39.4 18.8 %copy-start.5 = (bf16[128,1024]{1,0:T(8,128)(2,1)S(1)}, bf16[128,1024]{1,0:T(8,128)(2,1)}, u32[]{:S(2)}) copy-start(bf16[128,1024]{1,0:T(8,128)(2,1)} %wout.3) | copy-start | bytes 786436
  39.4 18.7 %all-to-all-start = ((bf16[32,4,256]{2,1,0:T(4,128)(2,1)}), bf16[32,4,256]{2,1,0:T(4,128)(2,1)S(1)}, u32[]{:S(2)}, u32[]{:S(2)}) async-start(bf16[32,4,256]{2,1,0:T(4,128)(2,1)} %get-tuple-element.29), calls=%async_computation | async-start | bytes 131072 | tf_op jit(solution)/shard_map/all_to_all | solution.py:271
  50.0 8.1 %copy-start.9 = (f32[2]{0:T(128)S(1)}, f32[2]{0:T(128)}, u32[]{:S(2)}) copy-start(f32[2]{0:T(128)} %scale.3) | copy-start | bytes 28
  60.5 10.9 %copy-start.8 = (f32[1024]{0:T(1024)S(1)}, f32[1024]{0:T(1024)}, u32[]{:S(2)}) copy-start(f32[1024]{0:T(1024)} %param.29) | copy-start | bytes 12292

commit v2 on v1

v2 whole, which is shorter than its diff:
```python
import functools

import jax
import jax.numpy as jnp
from jax import lax
from jax.experimental import pallas as pl
from jax.experimental.pallas import tpu as pltpu
from jax.sharding import PartitionSpec as P

HEAD = 64
POOL = 8
EPS = 1e-06
LOG2E = 1.4426950408889634
QCHUNK = 256
VMEM_LIMIT = 40 * 1024 * 1024
NT = (((1,), (1,)), ((), ()))
NN = (((1,), (0,)), ((), ()))
F32 = jnp.float32
BF16 = jnp.bfloat16


def mm(a, b, dims=NN):
    return lax.dot_general(a, b, dims, preferred_element_type=F32)


def rms_rows(value):
    return value * lax.rsqrt(jnp.mean(value * value, axis=-1, keepdims=True) + EPS)


def head_means(value):
    width = value.shape[1]
    i = lax.broadcasted_iota(jnp.int32, (width, width), 0) // HEAD
    j = lax.broadcasted_iota(jnp.int32, (width, width), 1) // HEAD
    ones = jnp.where(i == j, 1.0 / HEAD, 0.0).astype(BF16)
    return mm((value * value).astype(BF16), ones)


def low_lanes(shape):
    return lax.broadcasted_iota(jnp.int32, shape, 1) < HEAD


def level_row(level_ref, table_ref):
    table = table_ref[...]
    ids = lax.broadcasted_iota(jnp.int32, table.shape, 0)
    return jnp.sum(jnp.where(ids == level_ref[0], table, 0.0), axis=0, keepdims=True)


def gain_row(cond, ada_ref):
    return 1.0 + lax.dot_general(
        cond, ada_ref[...], NN, precision=lax.Precision.HIGHEST, preferred_element_type=F32
    )


def tile_kv(x, gain, wkv, valid):
    width = x.shape[1]
    xn = (rms_rows(x.astype(F32)) * gain).astype(BF16)
    proj = mm(xn, wkv)
    k = proj[:, :width]
    k = (k * lax.rsqrt(head_means(k) + EPS)).astype(BF16)
    v = proj[:, width:]
    low = low_lanes(v.shape)
    v0 = jnp.where(low, v, valid).astype(BF16)
    v1 = jnp.where(low, valid, v).astype(BF16)
    return xn, k, v0, v1


def attend_tile(q_refs, k, vs, acc_refs, first):
    for start in range(0, q_refs[0].shape[0], QCHUNK):
        rows = pl.ds(start, QCHUNK)
        for q_ref, v, acc_ref in zip(q_refs, vs, acc_refs):
            p = jnp.exp2(mm(q_ref[rows, :], k, NT)).astype(BF16)
            part = mm(p, v)
            if first:
                acc_ref[rows, :] = part
            else:
                acc_ref[rows, :] += part


def fetch(pairs, sems):
    copies = [pltpu.make_async_copy(src, dst, sems.at[i]) for i, (src, dst) in enumerate(pairs)]
    for copy in copies:
        copy.start()
    return copies


def own_kernel(
    level,
    scale_hbm,
    x_hbm,
    table_hbm,
    ada_hbm,
    wqkv_hbm,
    q0,
    q1,
    acc0,
    acc1,
    gain_out,
    cond_out,
    wkv_out,
    scale,
    x,
    table,
    ada,
    wqkv,
    sems,
):
    copies = fetch(
        (
            (table_hbm, table),
            (ada_hbm, ada),
            (x_hbm, x),
            (wqkv_hbm, wqkv),
            (scale_hbm, scale),
        ),
        sems,
    )
    for copy in copies:
        copy.wait()
    width = x.shape[1]
    cond = level_row(level, table)
    gain = gain_row(cond, ada)
    cond_out[...] = cond
    gain_out[...] = gain
    wkv = wqkv[:, width:]
    wkv_out[...] = wkv
    xn, k, v0, v1 = tile_kv(x[...], gain, wkv, 1.0)
    q = mm(xn, wqkv[:, :width])
    low = low_lanes(q.shape)
    factor = jnp.where(low, scale[0], scale[1]) * (LOG2E / HEAD)
    q = q * lax.rsqrt(head_means(q) + EPS) * factor
    q0[...] = jnp.where(low, q, 0.0).astype(BF16)
    q1[...] = jnp.where(low, 0.0, q).astype(BF16)
    attend_tile((q0, q1), k, (v0, v1), (acc0, acc1), True)


def more_tiles(which, tiles, gain, wkv, q_refs, acc_refs):
    row, col = lax.axis_index("row"), lax.axis_index("col")
    row_ok = jnp.where((row > 0) & (row < lax.axis_size("row") - 1), 1.0, 0.0)
    col_ok = jnp.where((col > 0) & (col < lax.axis_size("col") - 1), 1.0, 0.0)
    flags = {
        "col": (1.0, col_ok),
        "near": (1.0, 1.0, col_ok),
        "far": (row_ok, row_ok, row_ok * col_ok),
    }
    for at, valid in enumerate(flags[which]):
        _, k, v0, v1 = tile_kv(tiles[at][...], gain[...], wkv[...], valid)
        attend_tile(q_refs, k, (v0, v1), acc_refs, at == 0)


def col_kernel(a, b, gain, wkv, q0, q1, acc0, acc1):
    more_tiles("col", (a, b), gain, wkv, (q0, q1), (acc0, acc1))


def near_kernel(tiles, gain, wkv, q0, q1, acc0, acc1):
    more_tiles("near", [tiles.at[i] for i in range(3)], gain, wkv, (q0, q1), (acc0, acc1))


def far_kernel(
    tiles,
    gain,
    wkv,
    q0,
    q1,
    own0,
    own1,
    col0,
    col1,
    near0,
    near1,
    x_hbm,
    wout_hbm,
    post_hbm,
    wmerge_hbm,
    out_hbm,
    pooled,
    pooled_all,
    acc0,
    acc1,
    x,
    wout,
    post,
    wmerge,
    out,
    sems,
):
    copies = fetch(
        ((x_hbm, x), (wout_hbm, wout), (post_hbm, post), (wmerge_hbm, wmerge)), sems
    )
    more_tiles("far", [tiles.at[i] for i in range(3)], gain, wkv, (q0, q1), (acc0, acc1))
    for copy in copies:
        copy.wait()
    tokens, width = x.shape
    low = low_lanes((tokens, width))
    a0 = (own0[...] + col0[...]) + (near0[...] + acc0[...])
    a1 = (own1[...] + col1[...]) + (near1[...] + acc1[...])
    sums = pltpu.roll(jnp.where(low, a1, a0), HEAD, 1)
    attended = (jnp.where(low, a0, a1) / sums).astype(BF16)
    branch = mm(attended, wout[...])
    result = (x[...].astype(F32) + rms_rows(branch) * post[...]).astype(BF16)
    out[...] = result
    store = pltpu.make_async_copy(out, out_hbm, sems.at[4])
    store.start()
    side = 32
    group = lax.broadcasted_iota(jnp.int32, (16, tokens), 0)
    token = lax.broadcasted_iota(jnp.int32, (16, tokens), 1)
    i, j = token // side, token % side
    place = ((i % 2) * 2 + j % 2) * 4 + (i // (2 * POOL)) * 2 + j // (2 * POOL)
    pick = jnp.where(group == place, 1.0 / (POOL * POOL), 0.0).astype(BF16)
    means = mm(pick, result)
    high = means.astype(BF16)
    rest = (means - high.astype(F32)).astype(BF16)
    total = jnp.zeros((4, wmerge.shape[1]), F32)
    for part in range(4):
        w = wmerge[pl.ds(part * width, width), :]
        at = slice(4 * part, 4 * part + 4)
        total += mm(high[at], w) + mm(rest[at], w)
    total = total.astype(BF16)
    pooled[...] = total
    pooled_all[...] = jnp.broadcast_to(total[None], pooled_all.shape)
    store.wait()


def prepare_kernel(pooled, cond, ada, win, gain, coarse_in):
    gain[...] = gain_row(cond[...], ada)
    coarse_in[...] = mm(pooled[...], win[...])


def coarse_kernel(scale_hbm, tokens, gain, win, wqkv, wout, part_out, q_ref, scale, sems):
    (copy,) = fetch(((scale_hbm, scale),), sems)
    row = lax.axis_index("row")
    count = tokens.shape[0]
    rows_each = count // lax.axis_size("row")
    coarse_in = mm(tokens[...], win[...])
    cn = (rms_rows(coarse_in) * gain[...]).astype(BF16)
    qk = mm(cn, jnp.concatenate([wqkv[0], wqkv[1]], axis=1))
    width = wqkv.shape[2]
    k = qk[:, width:]
    v = mm(cn, wqkv[2])
    q_ref[...] = qk[:, :width]
    q = q_ref[pl.ds(pl.multiple_of(row * rows_each, rows_each), rows_each), :]
    copy.wait()
    low = low_lanes(q.shape)
    factor = jnp.where(low, scale[0], scale[1]) * (LOG2E / HEAD)
    q = q * lax.rsqrt(head_means(q) + EPS) * factor
    k = (k * lax.rsqrt(head_means(k) + EPS)).astype(BF16)
    wide = low_lanes(v.shape)
    v0 = jnp.where(wide, v, 1.0).astype(BF16)
    v1 = jnp.where(wide, 1.0, v).astype(BF16)
    q0 = jnp.where(low, q, 0.0).astype(BF16)
    q1 = jnp.where(low, 0.0, q).astype(BF16)
    a0 = mm(jnp.exp2(mm(q0, k, NT)).astype(BF16), v0)
    a1 = mm(jnp.exp2(mm(q1, k, NT)).astype(BF16), v1)
    sums = pltpu.roll(jnp.where(low, a1, a0), HEAD, 1)
    attended = (jnp.where(low, a0, a1) / sums).astype(BF16)
    part_out[...] = mm(attended, wout[...]).astype(BF16).reshape(part_out.shape)


def final_kernel(parts, coarse_in, post, out):
    branch = jnp.sum(parts[...].astype(F32), axis=0)
    result = (coarse_in[...] + rms_rows(branch) * post[...]).astype(BF16)
    each = out.shape[1]
    for at in range(out.shape[0]):
        out[at] = result[at * each : (at + 1) * each]


def call(kernel, out_shape, args, spaces, outs=None, scratch=(), flops=0, name=None):
    specs = {
        "s": pl.BlockSpec(memory_space=pltpu.SMEM),
        "v": pl.BlockSpec(memory_space=pltpu.VMEM),
        "h": pl.BlockSpec(memory_space=pltpu.HBM),
    }
    moved = sum(a.size * a.dtype.itemsize for a in args)
    args = [
        pltpu.with_memory_space_constraint(a, pltpu.HBM) if space == "h" else a
        for a, space in zip(args, spaces)
    ]
    return pl.pallas_call(
        kernel,
        out_shape=out_shape,
        in_specs=[specs[space] for space in spaces],
        out_specs=tuple(specs[space] for space in (outs or "v" * len(out_shape))),
        scratch_shapes=list(scratch),
        compiler_params=pltpu.CompilerParams(vmem_limit_bytes=VMEM_LIMIT),
        cost_estimate=pl.CostEstimate(flops=flops, bytes_accessed=moved, transcendentals=0),
        name=name,
    )(*args)


def body(
    image,
    noise_level,
    cond_table,
    ada_fine,
    fine_qkv,
    fine_scale,
    fine_out_w,
    fine_post,
    merge_w,
    coarse_in_w,
    ada_coarse,
    coarse_qkv,
    coarse_scale,
    coarse_out_w,
    coarse_post,
):
    shape = jax.ShapeDtypeStruct
    rows, cols, width = image.shape
    count = rows * cols
    n_row, n_col = lax.axis_size("row"), lax.axis_size("col")
    x = image.reshape(count, width)

    def swaps(n, odd):
        pairs = [(i, i + 1) for i in range(odd, n - 1, 2)]
        return pairs + [(j, i) for i, j in pairs]

    tile_flops = 4 * count * count * width * 4
    col_a = lax.ppermute(x, "col", swaps(n_col, 0))
    col_b = lax.ppermute(x, "col", swaps(n_col, 1))
    vmem, dma = pltpu.VMEM, pltpu.SemaphoreType.DMA
    accs = (shape((count, width), F32),) * 2
    q0, q1, own0, own1, gain, cond, wkv = call(
        own_kernel,
        (shape((count, width), BF16),) * 2
        + accs
        + (
            shape((1, width), F32),
            shape((1, cond_table.shape[1]), F32),
            shape((width, 2 * width), BF16),
        ),
        (noise_level, fine_scale, x, cond_table, ada_fine, fine_qkv),
        "shhhhh",
        scratch=[
            pltpu.SMEM(fine_scale.shape, F32),
            vmem(x.shape, BF16),
            vmem(cond_table.shape, F32),
            vmem(ada_fine.shape, F32),
            vmem(fine_qkv.shape, BF16),
            dma((5,)),
        ],
        flops=tile_flops,
        name="own_tile",
    )
    held, gain = lax.optimization_barrier((x, gain))
    three = jnp.stack([held, col_a, col_b])
    near = lax.ppermute(three, "row", swaps(n_row, 0))
    far = lax.ppermute(three, "row", swaps(n_row, 1))
    col0, col1 = call(
        col_kernel,
        accs,
        (col_a, col_b, gain, wkv, q0, q1),
        "vvvvvv",
        flops=2 * tile_flops,
        name="col_tiles",
    )
    near0, near1 = call(
        near_kernel,
        accs,
        (near, gain, wkv, q0, q1),
        "vvvvv",
        flops=3 * tile_flops,
        name="near_row_tiles",
    )
    devices = n_row * n_col
    merge_width = merge_w.shape[1]
    own = 4
    post = fine_post[None]
    fine_out, pooled, pooled_all = call(
        far_kernel,
        (
            shape((count, width), BF16),
            shape((own, merge_width), BF16),
            shape((devices, own, merge_width), BF16),
        ),
        (far, gain, wkv, q0, q1, own0, own1, col0, col1, near0, near1)
        + (x, fine_out_w, post, merge_w),
        "v" * 11 + "hhhh",
        outs="hvv",
        scratch=[vmem((count, width), F32)] * 2
        + [
            vmem(x.shape, BF16),
            vmem(fine_out_w.shape, BF16),
            vmem(post.shape, F32),
            vmem(merge_w.shape, BF16),
            vmem(x.shape, BF16),
            dma((5,)),
        ],
        flops=3 * tile_flops,
        name="far_row_tiles",
    )
    tokens = lax.all_to_all(pooled_all, ("row", "col"), 0, 0, tiled=True)
    coarse_width = coarse_in_w.shape[1]
    coarse_gain, coarse_in = call(
        prepare_kernel,
        (shape((1, coarse_width), F32), shape((own, coarse_width), F32)),
        (pooled, cond, ada_coarse, coarse_in_w),
        "vvvv",
        name="coarse_prepare",
    )
    (parts,) = call(
        coarse_kernel,
        (shape((n_col, own, coarse_width), BF16),),
        (
            coarse_scale,
            tokens.reshape(-1, merge_width),
            coarse_gain,
            coarse_in_w,
            coarse_qkv,
            coarse_out_w,
        ),
        "hvvvvv",
        scratch=[
            vmem((devices * own, coarse_qkv.shape[2]), F32),
            pltpu.SMEM(coarse_scale.shape, F32),
            dma((1,)),
        ],
        name="coarse",
    )
    parts = lax.all_to_all(parts, "col", 0, 0, tiled=True)
    pooled_rows, pooled_cols = rows // (2 * POOL), cols // (2 * POOL)
    (coarse_out,) = call(
        final_kernel,
        (shape((pooled_rows, pooled_cols, coarse_width), BF16),),
        (parts, coarse_in, coarse_post[None]),
        "vvv",
        name="coarse_out",
    )
    return fine_out.reshape(rows, cols, width), coarse_out


def solution(mesh):
    in_specs = (
        P(("noise", "row"), "col", None),
        P("noise"),
        P(),
        P(),
        P(),
        P(),
        P(),
        P(),
        P(),
        P(),
        P(),
        P(None, None, "col"),
        P("col"),
        P("col", None),
        P(),
    )
    out_specs = (P(("noise", "row"), "col", None), P(("noise", "row"), "col", None))
    return jax.shard_map(body, mesh=mesh, in_specs=in_specs, out_specs=out_specs, check_vma=False)
```

time: 72.6 us -> 71.9 us (level)
  local copies, waits for them, and re-layouts: 5.43 us -> 0.06 us
  Pallas kernels: 29.4 us -> 32.2 us
  waiting for transfers between devices: 8.08 us -> 9.27 us
  starting transfers between devices: 16.8 us -> 17.7 us
    unnamed x34 -> x12, local copies, waits for them, and re-layouts: 4.12 us -> 0.04 us
    pallas_call x6 -> x7, Pallas kernels: 29.4 us -> 32.2 us  [call(): pl.pallas_call(kernel, out_shape=out_shape, in_specs=[specs[space] for sp...]
    ppermute x1, waiting for transfers between devices: 0.01 us -> 1.19 us  [body(): col_a = lax.ppermute(x, 'col', swaps(n_col, 0))]
    all_to_all x1, starting transfers between devices: 9.94 us -> 10.9 us  [body(): tokens = lax.all_to_all(pooled_all, ('row', 'col'), 0, 0, tiled=True)]
  transfers between devices with their start and end apart: 5 -> 5, of which waited for: 1 -> 2; matrix products, arithmetic and copies ran while one was open for 1% -> 0% of each run, Pallas kernels for 24% -> 26%
where the time goes in v2:
time: 71.9 us; the launch traced here: 71.6 us
  Pallas kernels  32.2 us (45%)
  starting transfers between devices  17.7 us (25%)
  blocking collectives  10.8 us (15%)
  waiting for transfers between devices  9.27 us (13%)
  between operations  1.46 us (2%)
    pallas_call x7, Pallas kernels, call(): pl.pallas_call(kernel, out_shape=out_shape, in_specs=[specs[space] for sp...  32.2 us
    all_to_all x1, starting transfers between devices, body(): tokens = lax.all_to_all(pooled_all, ('row', 'col'), 0, 0, tiled=True)  10.9 us
    all_to_all x1, blocking collectives, body(): parts = lax.all_to_all(parts, 'col', 0, 0, tiled=True)  10.8 us
    all_to_all x1, waiting for transfers between devices, body(): tokens = lax.all_to_all(pooled_all, ('row', 'col'), 0, 0, tiled=True)  8.07 us
    ppermute x1, starting transfers between devices, body(): col_a = lax.ppermute(x, 'col', swaps(n_col, 0))  5.15 us
  transfers between devices with their start and end apart: 5, of which 2 were waited for; matrix products, arithmetic and copies ran while one was open for 0% of the time, Pallas kernels for 26%

profile of v2, /device:TPU:2, one launch (start us, length us, event | category | flops | bytes accessed | tf_op | source)
XLA Modules:
  0.0 71.6 jit_solution(208786409722432976)
XLA Ops:
  0.6 0.7 collective-permute-start.1
  1.3 5.2 %collective-permute-start = (bf16[1024,128]{1,0:T(8,128)(2,1)}, bf16[1024,128]{1,0:T(8,128)(2,1)S(1)}, u32[]{:S(2)}, u32[]{:S(2)}) collective-permute-start(bf16[1024,128]{1,0:T(8,128)(2,1)} %bitcast.11), channel_id=1, source_target_pairs={{0,1},{2,3},{4,5},{6,7},{1,0},{3,2},{5,4},{7,6},{8,9},{10,11},{12,... | collective-permute-start | bytes 786440 | tf_op jit(solution)/shard_map/ppermute | solution.py:317
  7.1 0.0 copy-start.5
  7.1 4.4 %own_tile.1 = (bf16[1024,128]{1,0:T(8,128)(2,1)S(1)}, bf16[1024,128]{1,0:T(8,128)(2,1)S(1)}, f32[1024,128]{1,0:T(8,128)S(1)}, f32[1024,128]{1,0:T(8,128)S(1)}, f...) custom-call(s32[1]{0:T(128)S(6)} %copy.17.level, f32[2]{0:T(128)} %scale_hbm.2, ...), custom_call_target="tpu_custom_call" | custom-call | flops 2147483648 | bytes 499724 | tf_op jit(solution)/shard_map/own_tile/pallas_call | solution.py:277
  11.5 0.0 collective-permute-done.1.b
  11.5 1.2 %collective-permute-done.a = bf16[1024,128]{1,0:T(8,128)(2,1)S(1)} collective-permute-done((bf16[1024,128]{1,0:T(8,128)(2,1)}, bf16[1024,128]{1,0:T(8,128)(2,1)S(1)}, u32[]{:S(2)}, u32[]{:S(2)}) %collective-permute-start) | collective-permute-done | bytes 262176 | tf_op jit(solution)/shard_map/ppermute | solution.py:317
  12.7 0.0 copy-done.5
  12.7 0.1 pad_maximum_fusion
  12.8 0.1 collective-permute-start.3
  12.9 0.9 %collective-permute-start.2 = (bf16[3,1024,128]{2,1,0:T(8,128)(2,1)S(1)}, bf16[3,1024,128]{2,1,0:T(8,128)(2,1)S(1)}, u32[]{:S(2)}, u32[]{:S(2)}) collective-permute-start(bf16[3,1024,128]{2,1,0:T(8,128)(2,1)S(1)} %pad_maximum_fusion), channel_id=1, source_target_pairs={{8,16},{16,8},{9,17},{17,9},{10,18},{18,10},{11,19},{19,11},{12,20... | collective-permute-start | bytes 2359304 | tf_op jit(solution)/shard_map/ppermute | solution.py:346
  13.8 5.4 %col_tiles.1 = (f32[1024,128]{1,0:T(8,128)S(1)}, f32[1024,128]{1,0:T(8,128)S(1)}) custom-call(bf16[1024,128]{1,0:T(8,128)(2,1)S(1)} %collective-permute-done.a, bf16[1024,128]{1,0:T(8,128)(2,1)S(1)} %collective-permute-done.1.b, f32[1,128]{1,0:T(1,128)S(1)} %get-tuple-element.22.gain, bf16[128,256]{1,0:T(8,128)(2,1)S(1)} %get-tuple-element.23.wkv, ...), custom_call_target="tpu_custom_call" | custom-call | flops 4294967296 | bytes 1114624 | tf_op jit(solution)/shard_map/col_tiles/pallas_call | solution.py:277
  19.2 0.0 collective-permute-done.3.tiles
  19.3 8.3 %near_row_tiles.1 = (f32[1024,128]{1,0:T(8,128)S(1)}, f32[1024,128]{1,0:T(8,128)S(1)}) custom-call(bf16[3,1024,128]{2,1,0:T(8,128)(2,1)S(1)} %collective-permute-done.3.tiles, f32[1,128]{1,0:T(1,128)S(1)} %get-tuple-element.22.gain, bf16[128,256]{1,0:T(8,128)(2,1)S(1)} %get-tuple-element.23.wkv, bf16[1024,128]{1,0:T(8,128)(2,1)S(1)} %get-tuple-element.24.q0, ...), custom_call_target="tpu_custom_call" | custom-call | flops 6442450944 | bytes 1376768 | tf_op jit(solution)/shard_map/near_row_tiles/pallas_call | solution.py:277
  27.5 0.0 collective-permute-done.2.tiles
  27.5 0.0 copy-start
  27.6 0.0 copy-start.1
  27.6 10.9 %far_row_tiles.1 = (bf16[1024,128]{1,0:T(8,128)(2,1)}, bf16[4,256]{1,0:T(4,128)(2,1)S(1)}, bf16[32,4,256]{2,1,0:T(4,128)(2,1)}) custom-call(bf16[3,1024,128]{2,1,0:T(8,128)(2,1)S(1)} %collective-permute-done.2.tiles, f32[1,128]{1,0:T(1,128)S(1)} %get-tuple-element.22.gain, bf16[128,256]{1,0:T(8,128)(2,1)S(1)} %get-tuple-element.23.wkv, ...), custom_call_target="tpu_custom_call" | custom-call | flops 6442450944 | bytes 5080064 | tf_op jit(solution)/shard_map/far_row_tiles/pallas_call | solution.py:277
  38.5 10.9 %all-to-all-start = ((bf16[32,4,256]{2,1,0:T(4,128)(2,1)}), bf16[32,4,256]{2,1,0:T(4,128)(2,1)S(1)}, u32[]{:S(2)}, u32[]{:S(2)}) async-start(bf16[32,4,256]{2,1,0:T(4,128)(2,1)} %get-tuple-element.33), calls=%async_computation | async-start | bytes 131072 | tf_op jit(solution)/shard_map/all_to_all | solution.py:390
  49.4 0.0 copy-done
  49.4 0.0 copy-done.1
  49.4 0.0 copy-start.2
  49.4 0.0 copy-start.3
  49.4 0.6 coarse_prepare.1
  50.0 8.1 %all-to-all-done = bf16[32,4,256]{2,1,0:T(4,128)(2,1)S(1)} async-done(((bf16[32,4,256]{2,1,0:T(4,128)(2,1)}), bf16[32,4,256]{2,1,0:T(4,128)(2,1)S(1)}, u32[]{:S(2)}, u32[]{:S(2)}) %all-to-all-start) | async-done | bytes 65568 | tf_op jit(solution)/shard_map/all_to_all | solution.py:390
  58.1 0.0 copy-done.2
  58.2 0.0 copy-done.3
  58.2 1.9 %coarse.1 = bf16[8,4,1024]{2,1,0:T(4,128)(2,1)S(1)} custom-call(f32[2]{0:T(128)} %scale_hbm.3, bf16[128,256]{1,0:T(8,128)(2,1)S(1)} %reshape.15.tokens, f32[1,1024]{1,0:T(1,128)S(1)} %get-tuple-element.36.gain, bf16[256,1024]{1,0:T(8,128)(2,1)S(1)} %copy-done, bf16[3,1024,128]{2,1,0:T(8,128)(2,1)S(1)} %copy-done.2, bf16[128,1024]{1,0:T(8,128)(2,1)S(1)} %copy-done.3), custom_call_target="tpu_custom_call" | custom-call | bytes 1642504 | tf_op jit(solution)/shard_map/coarse/pallas_call | solution.py:277
  60.1 0.0 copy-start.4
  60.1 10.8 %all_to_all.10.parts = bf16[8,4,1024]{2,1,0:T(4,128)(2,1)S(1)} all-to-all(bf16[8,4,1024]{2,1,0:T(4,128)(2,1)S(1)} %coarse.1), channel_id=1, replica_groups=mesh['noise'=8,'row'=4,'col'=8] {'col'}, dimensions={0} | all-to-all | bytes 131072 | tf_op jit(solution)/shard_map/all_to_all | solution.py:418
  70.8 0.0 copy-done.4
  70.8 0.7 %coarse_out.1 = bf16[2,2,1024]{2,1,0:T(2,128)(2,1)} custom-call(bf16[8,4,1024]{2,1,0:T(4,128)(2,1)S(1)} %all_to_all.10.parts, f32[4,1024]{1,0:T(4,128)S(1)} %get-tuple-element.37.coarse_in, f32[1,1024]{1,0:T(1,128)S(1)} %bitcast.9), custom_call_target="tpu_custom_call" | custom-call | bytes 86016 | tf_op jit(solution)/shard_map/coarse_out/pallas_call | solution.py:277
  (1 shorter events, 0.0 us)
Async XLA Ops:
  0.6 10.9 %collective-permute-start.1 = (bf16[1024,128]{1,0:T(8,128)(2,1)}, bf16[1024,128]{1,0:T(8,128)(2,1)S(1)}, u32[]{:S(2)}, u32[]{:S(2)}) collective-permute-start(bf16[1024,128]{1,0:T(8,128)(2,1)} %bitcast.10), channel_id=1, source_target_pairs={{1,2},{3,4},{5,6},{2,1},{4,3},{6,5},{9,10},{11,12},{13,14},{10,9},... | collective-permute-start | bytes 786440 | tf_op jit(solution)/shard_map/ppermute | solution.py:318
  1.3 11.4 %collective-permute-start = (bf16[1024,128]{1,0:T(8,128)(2,1)}, bf16[1024,128]{1,0:T(8,128)(2,1)S(1)}, u32[]{:S(2)}, u32[]{:S(2)}) collective-permute-start(bf16[1024,128]{1,0:T(8,128)(2,1)} %bitcast.11), channel_id=1, source_target_pairs={{0,1},{2,3},{4,5},{6,7},{1,0},{3,2},{5,4},{7,6},{8,9},{10,11},{12,... | collective-permute-start | bytes 786440 | tf_op jit(solution)/shard_map/ppermute | solution.py:317
  7.1 5.6 %copy-start.5 = (bf16[32,32,128]{2,1,0:T(8,128)(2,1)S(1)}, bf16[32,32,128]{2,1,0:T(8,128)(2,1)}, u32[]{:S(2)}) copy-start(bf16[32,32,128]{2,1,0:T(8,128)(2,1)} %param.15) | copy-start | bytes 786436
  12.8 6.4 %collective-permute-start.3 = (bf16[3,1024,128]{2,1,0:T(8,128)(2,1)S(1)}, bf16[3,1024,128]{2,1,0:T(8,128)(2,1)S(1)}, u32[]{:S(2)}, u32[]{:S(2)}) collective-permute-start(bf16[3,1024,128]{2,1,0:T(8,128)(2,1)S(1)} %pad_maximum_fusion), channel_id=1, source_target_pairs={{0,8},{16,24},{8,0},{24,16},{1,9},{17,25},{9,1},{25,17},{2,10},{18... | collective-permute-start | bytes 2359304 | tf_op jit(solution)/shard_map/ppermute | solution.py:345
  12.9 14.6 %collective-permute-start.2 = (bf16[3,1024,128]{2,1,0:T(8,128)(2,1)S(1)}, bf16[3,1024,128]{2,1,0:T(8,128)(2,1)S(1)}, u32[]{:S(2)}, u32[]{:S(2)}) collective-permute-start(bf16[3,1024,128]{2,1,0:T(8,128)(2,1)S(1)} %pad_maximum_fusion), channel_id=1, source_target_pairs={{8,16},{16,8},{9,17},{17,9},{10,18},{18,10},{11,19},{19,11},{12,20... | collective-permute-start | bytes 2359304 | tf_op jit(solution)/shard_map/ppermute | solution.py:346
  27.5 21.8 %copy-start = (bf16[256,1024]{1,0:T(8,128)(2,1)S(1)}, bf16[256,1024]{1,0:T(8,128)(2,1)}, u32[]{:S(2)}) copy-start(bf16[256,1024]{1,0:T(8,128)(2,1)} %win.3) | copy-start | bytes 1572868
  27.6 21.8 %copy-start.1 = (f32[256,1024]{1,0:T(8,128)S(1)}, f32[256,1024]{1,0:T(8,128)}, u32[]{:S(2)}) copy-start(f32[256,1024]{1,0:T(8,128)} %ada.1) | copy-start | bytes 3145732
  38.5 19.7 %all-to-all-start = ((bf16[32,4,256]{2,1,0:T(4,128)(2,1)}), bf16[32,4,256]{2,1,0:T(4,128)(2,1)S(1)}, u32[]{:S(2)}, u32[]{:S(2)}) async-start(bf16[32,4,256]{2,1,0:T(4,128)(2,1)} %get-tuple-element.33), calls=%async_computation | async-start | bytes 131072 | tf_op jit(solution)/shard_map/all_to_all | solution.py:390
  49.4 8.8 %copy-start.2 = (bf16[3,1024,128]{2,1,0:T(8,128)(2,1)S(1)}, bf16[3,1024,128]{2,1,0:T(8,128)(2,1)}, u32[]{:S(2)}) copy-start(bf16[3,1024,128]{2,1,0:T(8,128)(2,1)} %wqkv.1) | copy-start | bytes 2359300
  49.4 8.8 %copy-start.3 = (bf16[128,1024]{1,0:T(8,128)(2,1)S(1)}, bf16[128,1024]{1,0:T(8,128)(2,1)}, u32[]{:S(2)}) copy-start(bf16[128,1024]{1,0:T(8,128)(2,1)} %wout.1) | copy-start | bytes 786436
  60.1 10.8 %copy-start.4 = (f32[1024]{0:T(1024)S(1)}, f32[1024]{0:T(1024)}, u32[]{:S(2)}) copy-start(f32[1024]{0:T(1024)} %param.29) | copy-start | bytes 12292

commit v3 on v2

--- a/solution.py
+++ b/solution.py
@@ -53,7 +53,7 @@
 
 def tile_kv(x, gain, wkv, valid):
     width = x.shape[1]
-    xn = (rms_rows(x.astype(F32)) * gain).astype(BF16)
+    xn = (rms_rows(x.astype(F32)) * (gain * valid)).astype(BF16)
     proj = mm(xn, wkv)
     k = proj[:, :width]
     k = (k * lax.rsqrt(head_means(k) + EPS)).astype(BF16)
@@ -90,6 +90,8 @@
     table_hbm,
     ada_hbm,
     wqkv_hbm,
+    post_hbm,
+    near_tile,
     q0,
     q1,
     acc0,
@@ -97,6 +99,7 @@
     gain_out,
     cond_out,
     wkv_out,
+    post_out,
     scale,
     x,
     table,
@@ -111,6 +114,7 @@
             (x_hbm, x),
             (wqkv_hbm, wqkv),
             (scale_hbm, scale),
+            (post_hbm, post_out),
         ),
         sems,
     )
@@ -131,6 +135,8 @@
     q0[...] = jnp.where(low, q, 0.0).astype(BF16)
     q1[...] = jnp.where(low, 0.0, q).astype(BF16)
     attend_tile((q0, q1), k, (v0, v1), (acc0, acc1), True)
+    _, k, v0, v1 = tile_kv(near_tile[...], gain, wkv, 1.0)
+    attend_tile((q0, q1), k, (v0, v1), (acc0, acc1), False)
 
 
 def more_tiles(which, tiles, gain, wkv, q_refs, acc_refs):
@@ -139,7 +145,7 @@
     col_ok = jnp.where((col > 0) & (col < lax.axis_size("col") - 1), 1.0, 0.0)
     flags = {
         "col": (1.0, col_ok),
-        "near": (1.0, 1.0, col_ok),
+        "near": (1.0, col_ok),
         "far": (row_ok, row_ok, row_ok * col_ok),
     }
     for at, valid in enumerate(flags[which]):
@@ -152,7 +158,7 @@
 
 
 def near_kernel(tiles, gain, wkv, q0, q1, acc0, acc1):
-    more_tiles("near", [tiles.at[i] for i in range(3)], gain, wkv, (q0, q1), (acc0, acc1))
+    more_tiles("near", [tiles.at[i] for i in range(2)], gain, wkv, (q0, q1), (acc0, acc1))
 
 
 def far_kernel(
@@ -167,28 +173,17 @@
     col1,
     near0,
     near1,
-    x_hbm,
-    wout_hbm,
-    post_hbm,
-    wmerge_hbm,
-    out_hbm,
-    pooled,
-    pooled_all,
-    acc0,
-    acc1,
     x,
     wout,
     post,
     wmerge,
     out,
-    sems,
+    pooled,
+    pooled_all,
+    acc0,
+    acc1,
 ):
-    copies = fetch(
-        ((x_hbm, x), (wout_hbm, wout), (post_hbm, post), (wmerge_hbm, wmerge)), sems
-    )
     more_tiles("far", [tiles.at[i] for i in range(3)], gain, wkv, (q0, q1), (acc0, acc1))
-    for copy in copies:
-        copy.wait()
     tokens, width = x.shape
     low = low_lanes((tokens, width))
     a0 = (own0[...] + col0[...]) + (near0[...] + acc0[...])
@@ -198,8 +193,6 @@
     branch = mm(attended, wout[...])
     result = (x[...].astype(F32) + rms_rows(branch) * post[...]).astype(BF16)
     out[...] = result
-    store = pltpu.make_async_copy(out, out_hbm, sems.at[4])
-    store.start()
     side = 32
     group = lax.broadcasted_iota(jnp.int32, (16, tokens), 0)
     token = lax.broadcasted_iota(jnp.int32, (16, tokens), 1)
@@ -217,16 +210,16 @@
     total = total.astype(BF16)
     pooled[...] = total
     pooled_all[...] = jnp.broadcast_to(total[None], pooled_all.shape)
-    store.wait()
-
-
-def prepare_kernel(pooled, cond, ada, win, gain, coarse_in):
+
+
+def prepare_kernel(pooled, cond, ada, win, scale, gain, coarse_in, factor):
+    low = low_lanes(factor.shape)
+    factor[...] = jnp.where(low, scale[0:1, 0:1], scale[0:1, 1:2]) * (LOG2E / HEAD)
     gain[...] = gain_row(cond[...], ada)
     coarse_in[...] = mm(pooled[...], win[...])
 
 
-def coarse_kernel(scale_hbm, tokens, gain, win, wqkv, wout, part_out, q_ref, scale, sems):
-    (copy,) = fetch(((scale_hbm, scale),), sems)
+def coarse_kernel(factor, tokens, gain, win, wqkv, wout, part_out, q_ref):
     row = lax.axis_index("row")
     count = tokens.shape[0]
     rows_each = count // lax.axis_size("row")
@@ -238,10 +231,8 @@
     v = mm(cn, wqkv[2])
     q_ref[...] = qk[:, :width]
     q = q_ref[pl.ds(pl.multiple_of(row * rows_each, rows_each), rows_each), :]
-    copy.wait()
     low = low_lanes(q.shape)
-    factor = jnp.where(low, scale[0], scale[1]) * (LOG2E / HEAD)
-    q = q * lax.rsqrt(head_means(q) + EPS) * factor
+    q = q * lax.rsqrt(head_means(q) + EPS) * factor[...]
     k = (k * lax.rsqrt(head_means(k) + EPS)).astype(BF16)
     wide = low_lanes(v.shape)
     v0 = jnp.where(wide, v, 1.0).astype(BF16)
@@ -263,7 +254,7 @@
         out[at] = result[at * each : (at + 1) * each]
 
 
-def call(kernel, out_shape, args, spaces, outs=None, scratch=(), flops=0, name=None):
+def call(kernel, out_shape, args, spaces, scratch=(), flops=0, name=None):
     specs = {
         "s": pl.BlockSpec(memory_space=pltpu.SMEM),
         "v": pl.BlockSpec(memory_space=pltpu.VMEM),
@@ -278,7 +269,7 @@
         kernel,
         out_shape=out_shape,
         in_specs=[specs[space] for space in spaces],
-        out_specs=tuple(specs[space] for space in (outs or "v" * len(out_shape))),
+        out_specs=(specs["v"],) * len(out_shape),
         scratch_shapes=list(scratch),
         compiler_params=pltpu.CompilerParams(vmem_limit_bytes=VMEM_LIMIT),
         cost_estimate=pl.CostEstimate(flops=flops, bytes_accessed=moved, transcendentals=0),
@@ -310,15 +301,22 @@
     x = image.reshape(count, width)
 
     def swaps(n, odd):
-        pairs = [(i, i + 1) for i in range(odd, n - 1, 2)]
+        pairs = [(i, (i + 1) % n) for i in range(odd, n, 2)]
         return pairs + [(j, i) for i, j in pairs]
 
+    ring = 2 * n_row if lax.axis_size("noise") % 2 == 0 else n_row
+    far_pairs = [
+        (start + i, start + j)
+        for start in range(0, lax.axis_size("noise") * n_row, ring)
+        for i, j in swaps(ring, 1)
+    ]
     tile_flops = 4 * count * count * width * 4
+    near_tile = lax.ppermute(x, "row", swaps(n_row, 0))
     col_a = lax.ppermute(x, "col", swaps(n_col, 0))
     col_b = lax.ppermute(x, "col", swaps(n_col, 1))
     vmem, dma = pltpu.VMEM, pltpu.SemaphoreType.DMA
     accs = (shape((count, width), F32),) * 2
-    q0, q1, own0, own1, gain, cond, wkv = call(
+    q0, q1, own0, own1, gain, cond, wkv, post = call(
         own_kernel,
         (shape((count, width), BF16),) * 2
         + accs
@@ -326,24 +324,25 @@
             shape((1, width), F32),
             shape((1, cond_table.shape[1]), F32),
             shape((width, 2 * width), BF16),
+            shape((1, width), F32),
         ),
-        (noise_level, fine_scale, x, cond_table, ada_fine, fine_qkv),
-        "shhhhh",
+        (noise_level, fine_scale, x, cond_table, ada_fine, fine_qkv, fine_post[None], near_tile),
+        "shhhhhhv",
         scratch=[
             pltpu.SMEM(fine_scale.shape, F32),
             vmem(x.shape, BF16),
             vmem(cond_table.shape, F32),
             vmem(ada_fine.shape, F32),
             vmem(fine_qkv.shape, BF16),
-            dma((5,)),
+            dma((6,)),
         ],
-        flops=tile_flops,
+        flops=2 * tile_flops,
         name="own_tile",
     )
-    held, gain = lax.optimization_barrier((x, gain))
+    held, col_a, col_b, gain = lax.optimization_barrier((x, col_a, col_b, gain))
     three = jnp.stack([held, col_a, col_b])
-    near = lax.ppermute(three, "row", swaps(n_row, 0))
-    far = lax.ppermute(three, "row", swaps(n_row, 1))
+    near = lax.ppermute(jnp.stack([col_a, col_b]), "row", swaps(n_row, 0))
+    far = lax.ppermute(three, ("noise", "row"), far_pairs)
     col0, col1 = call(
         col_kernel,
         accs,
@@ -357,13 +356,12 @@
         accs,
         (near, gain, wkv, q0, q1),
         "vvvvv",
-        flops=3 * tile_flops,
+        flops=2 * tile_flops,
         name="near_row_tiles",
     )
     devices = n_row * n_col
     merge_width = merge_w.shape[1]
     own = 4
-    post = fine_post[None]
     fine_out, pooled, pooled_all = call(
         far_kernel,
         (
@@ -373,46 +371,38 @@
         ),
         (far, gain, wkv, q0, q1, own0, own1, col0, col1, near0, near1)
         + (x, fine_out_w, post, merge_w),
-        "v" * 11 + "hhhh",
-        outs="hvv",
-        scratch=[vmem((count, width), F32)] * 2
-        + [
-            vmem(x.shape, BF16),
-            vmem(fine_out_w.shape, BF16),
-            vmem(post.shape, F32),
-            vmem(merge_w.shape, BF16),
-            vmem(x.shape, BF16),
-            dma((5,)),
-        ],
+        "v" * 15,
+        scratch=[vmem((count, width), F32)] * 2,
         flops=3 * tile_flops,
         name="far_row_tiles",
     )
     tokens = lax.all_to_all(pooled_all, ("row", "col"), 0, 0, tiled=True)
     coarse_width = coarse_in_w.shape[1]
-    coarse_gain, coarse_in = call(
+    local_width = coarse_qkv.shape[2]
+    coarse_gain, coarse_in, factor = call(
         prepare_kernel,
-        (shape((1, coarse_width), F32), shape((own, coarse_width), F32)),
-        (pooled, cond, ada_coarse, coarse_in_w),
-        "vvvv",
+        (
+            shape((1, coarse_width), F32),
+            shape((own, coarse_width), F32),
+            shape((1, local_width), F32),
+        ),
+        (pooled, cond, ada_coarse, coarse_in_w, coarse_scale[None]),
+        "vvvvv",
         name="coarse_prepare",
     )
     (parts,) = call(
         coarse_kernel,
         (shape((n_col, own, coarse_width), BF16),),
         (
-            coarse_scale,
+            factor,
             tokens.reshape(-1, merge_width),
             coarse_gain,
             coarse_in_w,
             coarse_qkv,
             coarse_out_w,
         ),
-        "hvvvvv",
-        scratch=[
-            vmem((devices * own, coarse_qkv.shape[2]), F32),
-            pltpu.SMEM(coarse_scale.shape, F32),
-            dma((1,)),
-        ],
+        "vvvvvv",
+        scratch=[vmem((devices * own, local_width), F32)],
         name="coarse",
     )
     parts = lax.all_to_all(parts, "col", 0, 0, tiled=True)

time: 71.9 us -> 66.1 us (0.919)
  starting transfers between devices: 17.7 us -> 13.2 us
  Pallas kernels: 32.2 us -> 30.1 us
  local copies, waits for them, and re-layouts: 0.06 us -> 1.49 us
  waiting for transfers between devices: 9.27 us -> 8.43 us
    all_to_all x1, starting transfers between devices: 10.9 us -> 4.51 us  [body(): tokens = lax.all_to_all(pooled_all, ('row', 'col'), 0, 0, tiled=True)]
    ppermute x1, starting transfers between devices: 0.68 us -> 5.94 us  [body(): col_b = lax.ppermute(x, 'col', swaps(n_col, 1))]
    ppermute x1, starting transfers between devices: 5.15 us -> 0.01 us  [body(): col_a = lax.ppermute(x, 'col', swaps(n_col, 0))]
    pallas_call x7, Pallas kernels: 32.2 us -> 30.1 us  [call(): pl.pallas_call(kernel, out_shape=out_shape, in_specs=[specs[space] for sp...]
    ppermute x2 -> x3, starting transfers between devices: 0.98 us -> 2.78 us  [the longest x1 2.59 us: body(): far = lax.ppermute(three, ('noise', 'row'), far_pairs)]
    unnamed x12 -> x18, local copies, waits for them, and re-layouts: 0.04 us -> 1.47 us
  transfers between devices with their start and end apart: 5 -> 6, of which waited for: 2 -> 2; matrix products, arithmetic and copies ran while one was open for 0% -> 0% of each run, Pallas kernels for 26% -> 28%
where the time goes in v3:
time: 66.1 us; the launch traced here: 65.8 us
  Pallas kernels  30.1 us (46%)
  starting transfers between devices  13.2 us (20%)
  blocking collectives  10.9 us (16%)
  waiting for transfers between devices  8.43 us (13%)
  local copies, waits for them, and re-layouts  1.49 us (2%)
  between operations  1.47 us (2%)
    pallas_call x7, Pallas kernels, call(): pl.pallas_call(kernel, out_shape=out_shape, in_specs=[specs[space] for sp...  30.1 us
    all_to_all x1, blocking collectives, body(): parts = lax.all_to_all(parts, 'col', 0, 0, tiled=True)  10.9 us
    all_to_all x1, waiting for transfers between devices, body(): tokens = lax.all_to_all(pooled_all, ('row', 'col'), 0, 0, tiled=True)  7.45 us
    ppermute x1, starting transfers between devices, body(): col_b = lax.ppermute(x, 'col', swaps(n_col, 1))  5.94 us
    all_to_all x1, starting transfers between devices, body(): tokens = lax.all_to_all(pooled_all, ('row', 'col'), 0, 0, tiled=True)  4.51 us
    ppermute x1, starting transfers between devices, body(): far = lax.ppermute(three, ('noise', 'row'), far_pairs)  2.59 us
    unnamed x18, local copies, waits for them, and re-layouts  1.47 us
  transfers between devices with their start and end apart: 6, of which 2 were waited for; matrix products, arithmetic and copies ran while one was open for 0% of the time, Pallas kernels for 28%

profile of v3, /device:TPU:2, one launch (start us, length us, event | category | flops | bytes accessed | tf_op | source)
XLA Modules:
  0.0 65.8 jit_solution(11320271194335538394)
XLA Ops:
  0.6 0.1 collective-permute-start.2
  0.7 5.9 %collective-permute-start.1 = (bf16[1024,128]{1,0:T(8,128)(2,1)}, bf16[1024,128]{1,0:T(8,128)(2,1)S(1)}, u32[]{:S(2)}, u32[]{:S(2)}) collective-permute-start(bf16[1024,128]{1,0:T(8,128)(2,1)} %bitcast.13), channel_id=1, source_target_pairs={{1,2},{3,4},{5,6},{7,0},{2,1},{4,3},{6,5},{0,7},{9,10},{11,12},{13... | collective-permute-start | bytes 786440 | tf_op jit(solution)/shard_map/ppermute | solution.py:316
  6.7 0.0 collective-permute-start
  7.3 0.0 collective-permute-done.2.near_tile
  7.3 6.9 %own_tile.1 = (bf16[1024,128]{1,0:T(8,128)(2,1)S(1)}, bf16[1024,128]{1,0:T(8,128)(2,1)S(1)}, f32[1024,128]{1,0:T(8,128)S(1)}, f32[1024,128]{1,0:T(8,128)S(1)}, f...) custom-call(s32[1]{0:T(128)S(6)} %copy.17.level, ...), custom_call_target="tpu_custom_call" | custom-call | flops 4294967296 | bytes 762380 | tf_op jit(solution)/shard_map/own_tile/pallas_call | solution.py:268
  14.3 0.0 collective-permute-done.1.b
  14.3 1.0 %collective-permute-done.a = bf16[1024,128]{1,0:T(8,128)(2,1)S(1)} collective-permute-done((bf16[1024,128]{1,0:T(8,128)(2,1)}, bf16[1024,128]{1,0:T(8,128)(2,1)S(1)}, u32[]{:S(2)}, u32[]{:S(2)}) %collective-permute-start) | collective-permute-done | bytes 262176 | tf_op jit(solution)/shard_map/ppermute | solution.py:315
  15.2 0.0 copy-start.4
  15.2 0.1 pad_maximum_fusion.1
  15.3 0.1 collective-permute-start.4
  15.4 0.8 %copy-done.4 = bf16[32,32,128]{2,1,0:T(8,128)(2,1)S(1)} copy-done((bf16[32,32,128]{2,1,0:T(8,128)(2,1)S(1)}, bf16[32,32,128]{2,1,0:T(8,128)(2,1)}, u32[]{:S(2)}) %copy-start.4) | copy-done | bytes 262168
  16.2 0.1 pad_maximum_fusion
  16.3 2.6 %collective-permute-start.3 = (bf16[3,1024,128]{2,1,0:T(8,128)(2,1)S(1)}, bf16[3,1024,128]{2,1,0:T(8,128)(2,1)S(1)}, u32[]{:S(2)}, u32[]{:S(2)}) collective-permute-start(bf16[3,1024,128]{2,1,0:T(8,128)(2,1)S(1)} %pad_maximum_fusion), channel_id=1, source_target_pairs={{8,16},{24,32},{40,48},{56,0},{16,8},{32,24},{48,40},{0,56},{72,80... | collective-permute-start | bytes 2359304 | tf_op jit(solution)/shard_map/ppermute | solution.py:345
  18.9 5.4 %col_tiles.1 = (f32[1024,128]{1,0:T(8,128)S(1)}, f32[1024,128]{1,0:T(8,128)S(1)}) custom-call(bf16[1024,128]{1,0:T(8,128)(2,1)S(1)} %collective-permute-done.a, bf16[1024,128]{1,0:T(8,128)(2,1)S(1)} %collective-permute-done.1.b, f32[1,128]{1,0:T(1,128)S(1)} %get-tuple-element.28.gain, bf16[128,256]{1,0:T(8,128)(2,1)S(1)} %get-tuple-element.29.wkv, ...), custom_call_target="tpu_custom_call" | custom-call | flops 4294967296 | bytes 1114624 | tf_op jit(solution)/shard_map/col_tiles/pallas_call | solution.py:268
  24.3 0.0 copy-start.7
  24.3 0.0 copy-start.8
  24.3 0.0 collective-permute-done.4.tiles
  24.4 5.4 %near_row_tiles.1 = (f32[1024,128]{1,0:T(8,128)S(1)}, f32[1024,128]{1,0:T(8,128)S(1)}) custom-call(bf16[2,1024,128]{2,1,0:T(8,128)(2,1)S(1)} %collective-permute-done.4.tiles, f32[1,128]{1,0:T(1,128)S(1)} %get-tuple-element.28.gain, bf16[128,256]{1,0:T(8,128)(2,1)S(1)} %get-tuple-element.29.wkv, bf16[1024,128]{1,0:T(8,128)(2,1)S(1)} %get-tuple-element.30.q0, ...), custom_call_target="tpu_custom_call" | custom-call | flops 4294967296 | bytes 1114624 | tf_op jit(solution)/shard_map/near_row_tiles/pallas_call | solution.py:268
  29.8 0.0 collective-permute-done.3.tiles
  29.8 0.0 copy-done.7
  29.8 0.0 copy-done.8
  29.8 0.0 copy-start
  29.8 0.0 copy-start.1
  29.8 9.7 %far_row_tiles.1 = (bf16[1024,128]{1,0:T(8,128)(2,1)}, bf16[4,256]{1,0:T(4,128)(2,1)S(1)}, bf16[32,4,256]{2,1,0:T(4,128)(2,1)}) custom-call(bf16[3,1024,128]{2,1,0:T(8,128)(2,1)S(1)} %collective-permute-done.3.tiles, f32[1,128]{1,0:T(1,128)S(1)} %get-tuple-element.28.gain, bf16[128,256]{1,0:T(8,128)(2,1)S(1)} %get-tuple-element.29.wkv, ...), custom_call_target="tpu_custom_call" | custom-call | flops 6442450944 | bytes 5080064 | tf_op jit(solution)/shard_map/far_row_tiles/pallas_call | solution.py:268
  39.5 4.5 %all-to-all-start = ((bf16[32,4,256]{2,1,0:T(4,128)(2,1)}), bf16[32,4,256]{2,1,0:T(4,128)(2,1)S(1)}, u32[]{:S(2)}, u32[]{:S(2)}) async-start(bf16[32,4,256]{2,1,0:T(4,128)(2,1)} %get-tuple-element.43), calls=%async_computation | async-start | bytes 131072 | tf_op jit(solution)/shard_map/all_to_all | solution.py:379
  44.0 0.0 copy-start.6
  44.1 0.0 copy-done
  44.1 0.0 copy-done.1
  44.1 0.6 copy-done.6
  44.7 0.0 copy-start.2
  44.7 0.0 copy-start.3
  44.7 0.6 coarse_prepare.1
  45.3 7.5 %all-to-all-done = bf16[32,4,256]{2,1,0:T(4,128)(2,1)S(1)} async-done(((bf16[32,4,256]{2,1,0:T(4,128)(2,1)}), bf16[32,4,256]{2,1,0:T(4,128)(2,1)S(1)}, u32[]{:S(2)}, u32[]{:S(2)}) %all-to-all-start) | async-done | bytes 65568 | tf_op jit(solution)/shard_map/all_to_all | solution.py:379
  52.8 0.0 copy-done.2
  52.8 0.0 copy-done.3
  52.8 1.3 %coarse.1 = bf16[8,4,1024]{2,1,0:T(4,128)(2,1)S(1)} custom-call(f32[1,128]{1,0:T(1,128)S(1)} %get-tuple-element.42.factor, bf16[128,256]{1,0:T(8,128)(2,1)S(1)} %reshape.15.tokens, f32[1,1024]{1,0:T(1,128)S(1)} %get-tuple-element.44.gain, bf16[256,1024]{1,0:T(8,128)(2,1)S(1)} %copy-done, bf16[3,1024,128]{2,1,0:T(8,128)(2,1)S(1)} %copy-done.2, ...), custom_call_target="tpu_custom_call" | custom-call | bytes 1643008 | tf_op jit(solution)/shard_map/coarse/pallas_call | solution.py:268
  54.2 0.0 copy-start.5
  54.2 10.9 %all_to_all.10.parts = bf16[8,4,1024]{2,1,0:T(4,128)(2,1)S(1)} all-to-all(bf16[8,4,1024]{2,1,0:T(4,128)(2,1)S(1)} %coarse.1), channel_id=1, replica_groups=mesh['noise'=8,'row'=4,'col'=8] {'col'}, dimensions={0} | all-to-all | bytes 131072 | tf_op jit(solution)/shard_map/all_to_all | solution.py:408
  65.1 0.0 copy-done.5
  65.1 0.7 %coarse_out.1 = bf16[2,2,1024]{2,1,0:T(2,128)(2,1)} custom-call(bf16[8,4,1024]{2,1,0:T(4,128)(2,1)S(1)} %all_to_all.10.parts, f32[4,1024]{1,0:T(4,128)S(1)} %get-tuple-element.45.coarse_in, f32[1,1024]{1,0:T(1,128)S(1)} %bitcast.18), custom_call_target="tpu_custom_call" | custom-call | bytes 86016 | tf_op jit(solution)/shard_map/coarse_out/pallas_call | solution.py:268
  (1 shorter events, 0.0 us)
Async XLA Ops:
  0.6 6.7 %collective-permute-start.2 = (bf16[1024,128]{1,0:T(8,128)(2,1)}, bf16[1024,128]{1,0:T(8,128)(2,1)S(1)}, u32[]{:S(2)}, u32[]{:S(2)}) collective-permute-start(bf16[1024,128]{1,0:T(8,128)(2,1)} %bitcast.12), channel_id=1, source_target_pairs={{0,8},{16,24},{8,0},{24,16},{1,9},{17,25},{9,1},{25,17},{2,10},{18... | collective-permute-start | bytes 786440 | tf_op jit(solution)/shard_map/ppermute | solution.py:314
  0.7 13.5 %collective-permute-start.1 = (bf16[1024,128]{1,0:T(8,128)(2,1)}, bf16[1024,128]{1,0:T(8,128)(2,1)S(1)}, u32[]{:S(2)}, u32[]{:S(2)}) collective-permute-start(bf16[1024,128]{1,0:T(8,128)(2,1)} %bitcast.13), channel_id=1, source_target_pairs={{1,2},{3,4},{5,6},{7,0},{2,1},{4,3},{6,5},{0,7},{9,10},{11,12},{13... | collective-permute-start | bytes 786440 | tf_op jit(solution)/shard_map/ppermute | solution.py:316
  6.7 8.6 %collective-permute-start = (bf16[1024,128]{1,0:T(8,128)(2,1)}, bf16[1024,128]{1,0:T(8,128)(2,1)S(1)}, u32[]{:S(2)}, u32[]{:S(2)}) collective-permute-start(bf16[1024,128]{1,0:T(8,128)(2,1)} %bitcast.14), channel_id=1, source_target_pairs={{0,1},{2,3},{4,5},{6,7},{1,0},{3,2},{5,4},{7,6},{8,9},{10,11},{12,... | collective-permute-start | bytes 786440 | tf_op jit(solution)/shard_map/ppermute | solution.py:315
  15.2 1.0 %copy-start.4 = (bf16[32,32,128]{2,1,0:T(8,128)(2,1)S(1)}, bf16[32,32,128]{2,1,0:T(8,128)(2,1)}, u32[]{:S(2)}) copy-start(bf16[32,32,128]{2,1,0:T(8,128)(2,1)} %param.15) | copy-start | bytes 786436
  15.3 9.0 %collective-permute-start.4 = (bf16[2,1024,128]{2,1,0:T(8,128)(2,1)S(1)}, bf16[2,1024,128]{2,1,0:T(8,128)(2,1)S(1)}, u32[]{:S(2)}, u32[]{:S(2)}) collective-permute-start(bf16[2,1024,128]{2,1,0:T(8,128)(2,1)S(1)} %pad_maximum_fusion.1), channel_id=1, source_target_pairs={{0,8},{16,24},{8,0},{24,16},{1,9},{17,25},{9,1},{25,17},{2,10},{18... | collective-permute-start | bytes 1572872 | tf_op jit(solution)/shard_map/ppermute | solution.py:344
  16.3 13.5 %collective-permute-start.3 = (bf16[3,1024,128]{2,1,0:T(8,128)(2,1)S(1)}, bf16[3,1024,128]{2,1,0:T(8,128)(2,1)S(1)}, u32[]{:S(2)}, u32[]{:S(2)}) collective-permute-start(bf16[3,1024,128]{2,1,0:T(8,128)(2,1)S(1)} %pad_maximum_fusion), channel_id=1, source_target_pairs={{8,16},{24,32},{40,48},{56,0},{16,8},{32,24},{48,40},{0,56},{72,80... | collective-permute-start | bytes 2359304 | tf_op jit(solution)/shard_map/ppermute | solution.py:345
  24.3 5.5 %copy-start.7 = (bf16[512,256]{1,0:T(8,128)(2,1)S(1)}, bf16[512,256]{1,0:T(8,128)(2,1)}, u32[]{:S(2)}) copy-start(bf16[512,256]{1,0:T(8,128)(2,1)} %wmerge.1) | copy-start | bytes 786436
  24.3 5.5 %copy-start.8 = (bf16[128,128]{1,0:T(8,128)(2,1)S(1)}, bf16[128,128]{1,0:T(8,128)(2,1)}, u32[]{:S(2)}) copy-start(bf16[128,128]{1,0:T(8,128)(2,1)} %wout.2) | copy-start | bytes 98308
  29.8 14.2 %copy-start = (bf16[256,1024]{1,0:T(8,128)(2,1)S(1)}, bf16[256,1024]{1,0:T(8,128)(2,1)}, u32[]{:S(2)}) copy-start(bf16[256,1024]{1,0:T(8,128)(2,1)} %win.3) | copy-start | bytes 1572868
  29.8 14.2 %copy-start.1 = (f32[256,1024]{1,0:T(8,128)S(1)}, f32[256,1024]{1,0:T(8,128)}, u32[]{:S(2)}) copy-start(f32[256,1024]{1,0:T(8,128)} %ada.1) | copy-start | bytes 3145732
  39.5 13.3 %all-to-all-start = ((bf16[32,4,256]{2,1,0:T(4,128)(2,1)}), bf16[32,4,256]{2,1,0:T(4,128)(2,1)S(1)}, u32[]{:S(2)}, u32[]{:S(2)}) async-start(bf16[32,4,256]{2,1,0:T(4,128)(2,1)} %get-tuple-element.43), calls=%async_computation | async-start | bytes 131072 | tf_op jit(solution)/shard_map/all_to_all | solution.py:379
  44.0 0.7 %copy-start.6 = (f32[2]{0:T(128)S(1)}, f32[2]{0:T(128)}, u32[]{:S(2)}) copy-start(f32[2]{0:T(128)} %param.27) | copy-start | bytes 28
  44.7 8.1 %copy-start.2 = (bf16[3,1024,128]{2,1,0:T(8,128)(2,1)S(1)}, bf16[3,1024,128]{2,1,0:T(8,128)(2,1)}, u32[]{:S(2)}) copy-start(bf16[3,1024,128]{2,1,0:T(8,128)(2,1)} %wqkv.1) | copy-start | bytes 2359300
  44.7 8.1 %copy-start.3 = (bf16[128,1024]{1,0:T(8,128)(2,1)S(1)}, bf16[128,1024]{1,0:T(8,128)(2,1)}, u32[]{:S(2)}) copy-start(bf16[128,1024]{1,0:T(8,128)(2,1)} %wout.3) | copy-start | bytes 786436
  54.2 10.9 %copy-start.5 = (f32[1024]{0:T(1024)S(1)}, f32[1024]{0:T(1024)}, u32[]{:S(2)}) copy-start(f32[1024]{0:T(1024)} %param.29) | copy-start | bytes 12292

commit v4 on v3

--- a/solution.py
+++ b/solution.py
@@ -27,12 +27,14 @@
     return value * lax.rsqrt(jnp.mean(value * value, axis=-1, keepdims=True) + EPS)
 
 
-def head_means(value):
-    width = value.shape[1]
-    i = lax.broadcasted_iota(jnp.int32, (width, width), 0) // HEAD
-    j = lax.broadcasted_iota(jnp.int32, (width, width), 1) // HEAD
-    ones = jnp.where(i == j, 1.0 / HEAD, 0.0).astype(BF16)
-    return mm((value * value).astype(BF16), ones)
+def head_rms(value):
+    low = low_lanes(value.shape)
+    square = value * value
+    first = jnp.sum(jnp.where(low, square, 0.0), axis=-1, keepdims=True)
+    second = jnp.sum(jnp.where(low, 0.0, square), axis=-1, keepdims=True)
+    first = lax.rsqrt(first * (1.0 / HEAD) + EPS)
+    second = lax.rsqrt(second * (1.0 / HEAD) + EPS)
+    return value * jnp.where(low, first, second)
 
 
 def low_lanes(shape):
@@ -55,8 +57,7 @@
     width = x.shape[1]
     xn = (rms_rows(x.astype(F32)) * (gain * valid)).astype(BF16)
     proj = mm(xn, wkv)
-    k = proj[:, :width]
-    k = (k * lax.rsqrt(head_means(k) + EPS)).astype(BF16)
+    k = head_rms(proj[:, :width]).astype(BF16)
     v = proj[:, width:]
     low = low_lanes(v.shape)
     v0 = jnp.where(low, v, valid).astype(BF16)
@@ -122,7 +123,10 @@
         copy.wait()
     width = x.shape[1]
     cond = level_row(level, table)
-    gain = gain_row(cond, ada)
+    turned = table[...].T
+    ids = lax.broadcasted_iota(jnp.int32, turned.shape, 1)
+    column = jnp.sum(jnp.where(ids == level[0], turned, 0.0), axis=1, keepdims=True)
+    gain = 1.0 + jnp.sum(column * ada[...], axis=0, keepdims=True)
     cond_out[...] = cond
     gain_out[...] = gain
     wkv = wqkv[:, width:]
@@ -131,12 +135,12 @@
     q = mm(xn, wqkv[:, :width])
     low = low_lanes(q.shape)
     factor = jnp.where(low, scale[0], scale[1]) * (LOG2E / HEAD)
-    q = q * lax.rsqrt(head_means(q) + EPS) * factor
+    q = head_rms(q) * factor
     q0[...] = jnp.where(low, q, 0.0).astype(BF16)
     q1[...] = jnp.where(low, 0.0, q).astype(BF16)
+    _, near_k, near_v0, near_v1 = tile_kv(near_tile[...], gain, wkv, 1.0)
     attend_tile((q0, q1), k, (v0, v1), (acc0, acc1), True)
-    _, k, v0, v1 = tile_kv(near_tile[...], gain, wkv, 1.0)
-    attend_tile((q0, q1), k, (v0, v1), (acc0, acc1), False)
+    attend_tile((q0, q1), near_k, (near_v0, near_v1), (acc0, acc1), False)
 
 
 def more_tiles(which, tiles, gain, wkv, q_refs, acc_refs):
@@ -148,8 +152,10 @@
         "near": (1.0, col_ok),
         "far": (row_ok, row_ok, row_ok * col_ok),
     }
-    for at, valid in enumerate(flags[which]):
-        _, k, v0, v1 = tile_kv(tiles[at][...], gain[...], wkv[...], valid)
+    held = [
+        tile_kv(tile[...], gain[...], wkv[...], valid) for tile, valid in zip(tiles, flags[which])
+    ]
+    for at, (_, k, v0, v1) in enumerate(held):
         attend_tile(q_refs, k, (v0, v1), acc_refs, at == 0)
 
 
@@ -232,8 +238,8 @@
     q_ref[...] = qk[:, :width]
     q = q_ref[pl.ds(pl.multiple_of(row * rows_each, rows_each), rows_each), :]
     low = low_lanes(q.shape)
-    q = q * lax.rsqrt(head_means(q) + EPS) * factor[...]
-    k = (k * lax.rsqrt(head_means(k) + EPS)).astype(BF16)
+    q = head_rms(q) * factor[...]
+    k = head_rms(k).astype(BF16)
     wide = low_lanes(v.shape)
     v0 = jnp.where(wide, v, 1.0).astype(BF16)
     v1 = jnp.where(wide, 1.0, v).astype(BF16)

time: 66.1 us -> 65 us (0.983)
  Pallas kernels: 30.1 us -> 28.9 us
    pallas_call x7, Pallas kernels: 30.1 us -> 28.9 us  [call(): pl.pallas_call(kernel, out_shape=out_shape, in_specs=[specs[space] for sp...]
  transfers between devices with their start and end apart: 6 -> 6, of which waited for: 2 -> 2; matrix products, arithmetic and copies ran while one was open for 0% -> 0% of each run, Pallas kernels for 28% -> 27%
where the time goes in v4:
time: 65 us; the launch traced here: 64.8 us
  Pallas kernels  28.9 us (44%)
  starting transfers between devices  13.2 us (20%)
  blocking collectives  10.9 us (17%)
  waiting for transfers between devices  8.64 us (13%)
  local copies, waits for them, and re-layouts  1.49 us (2%)
  between operations  1.47 us (2%)
    pallas_call x7, Pallas kernels, call(): pl.pallas_call(kernel, out_shape=out_shape, in_specs=[specs[space] for sp...  28.9 us
    all_to_all x1, blocking collectives, body(): parts = lax.all_to_all(parts, 'col', 0, 0, tiled=True)  10.9 us
    all_to_all x1, waiting for transfers between devices, body(): tokens = lax.all_to_all(pooled_all, ('row', 'col'), 0, 0, tiled=True)  7.45 us
    ppermute x1, starting transfers between devices, body(): col_b = lax.ppermute(x, 'col', swaps(n_col, 1))  5.94 us
    all_to_all x1, starting transfers between devices, body(): tokens = lax.all_to_all(pooled_all, ('row', 'col'), 0, 0, tiled=True)  4.5 us
    ppermute x1, starting transfers between devices, body(): far = lax.ppermute(three, ('noise', 'row'), far_pairs)  2.59 us
    unnamed x18, local copies, waits for them, and re-layouts  1.47 us
  transfers between devices with their start and end apart: 6, of which 2 were waited for; matrix products, arithmetic and copies ran while one was open for 0% of the time, Pallas kernels for 27%

profile of v4, /device:TPU:2, one launch (start us, length us, event | category | flops | bytes accessed | tf_op | source)
XLA Modules:
  0.0 64.8 jit_solution(4675931489623832634)
XLA Ops:
  0.6 0.1 collective-permute-start.2
  0.7 5.9 %collective-permute-start.1 = (bf16[1024,128]{1,0:T(8,128)(2,1)}, bf16[1024,128]{1,0:T(8,128)(2,1)S(1)}, u32[]{:S(2)}, u32[]{:S(2)}) collective-permute-start(bf16[1024,128]{1,0:T(8,128)(2,1)} %bitcast.13), channel_id=1, source_target_pairs={{1,2},{3,4},{5,6},{7,0},{2,1},{4,3},{6,5},{0,7},{9,10},{11,12},{13... | collective-permute-start | bytes 786440 | tf_op jit(solution)/shard_map/ppermute | solution.py:322
  6.7 0.0 collective-permute-start
  7.3 0.0 collective-permute-done.2.near_tile
  7.3 6.7 %own_tile.1 = (bf16[1024,128]{1,0:T(8,128)(2,1)S(1)}, bf16[1024,128]{1,0:T(8,128)(2,1)S(1)}, f32[1024,128]{1,0:T(8,128)S(1)}, f32[1024,128]{1,0:T(8,128)S(1)}, f...) custom-call(s32[1]{0:T(128)S(6)} %copy.17.level, ...), custom_call_target="tpu_custom_call" | custom-call | flops 4294967296 | bytes 762380 | tf_op jit(solution)/shard_map/own_tile/pallas_call | solution.py:274
  14.1 0.0 collective-permute-done.1.b
  14.1 1.2 %collective-permute-done.a = bf16[1024,128]{1,0:T(8,128)(2,1)S(1)} collective-permute-done((bf16[1024,128]{1,0:T(8,128)(2,1)}, bf16[1024,128]{1,0:T(8,128)(2,1)S(1)}, u32[]{:S(2)}, u32[]{:S(2)}) %collective-permute-start) | collective-permute-done | bytes 262176 | tf_op jit(solution)/shard_map/ppermute | solution.py:321
  15.2 0.0 copy-start.4
  15.2 0.1 pad_maximum_fusion.1
  15.3 0.1 collective-permute-start.4
  15.4 0.8 %copy-done.4 = bf16[32,32,128]{2,1,0:T(8,128)(2,1)S(1)} copy-done((bf16[32,32,128]{2,1,0:T(8,128)(2,1)S(1)}, bf16[32,32,128]{2,1,0:T(8,128)(2,1)}, u32[]{:S(2)}) %copy-start.4) | copy-done | bytes 262168
  16.2 0.1 pad_maximum_fusion
  16.3 2.6 %collective-permute-start.3 = (bf16[3,1024,128]{2,1,0:T(8,128)(2,1)S(1)}, bf16[3,1024,128]{2,1,0:T(8,128)(2,1)S(1)}, u32[]{:S(2)}, u32[]{:S(2)}) collective-permute-start(bf16[3,1024,128]{2,1,0:T(8,128)(2,1)S(1)} %pad_maximum_fusion), channel_id=1, source_target_pairs={{8,16},{24,32},{40,48},{56,0},{16,8},{32,24},{48,40},{0,56},{72,80... | collective-permute-start | bytes 2359304 | tf_op jit(solution)/shard_map/ppermute | solution.py:351
  18.9 5.2 %col_tiles.1 = (f32[1024,128]{1,0:T(8,128)S(1)}, f32[1024,128]{1,0:T(8,128)S(1)}) custom-call(bf16[1024,128]{1,0:T(8,128)(2,1)S(1)} %collective-permute-done.a, bf16[1024,128]{1,0:T(8,128)(2,1)S(1)} %collective-permute-done.1.b, f32[1,128]{1,0:T(1,128)S(1)} %get-tuple-element.28.gain, bf16[128,256]{1,0:T(8,128)(2,1)S(1)} %get-tuple-element.29.wkv, ...), custom_call_target="tpu_custom_call" | custom-call | flops 4294967296 | bytes 1114624 | tf_op jit(solution)/shard_map/col_tiles/pallas_call | solution.py:274
  24.1 0.0 copy-start.7
  24.1 0.0 copy-start.8
  24.1 0.0 collective-permute-done.4.tiles
  24.1 5.2 %near_row_tiles.1 = (f32[1024,128]{1,0:T(8,128)S(1)}, f32[1024,128]{1,0:T(8,128)S(1)}) custom-call(bf16[2,1024,128]{2,1,0:T(8,128)(2,1)S(1)} %collective-permute-done.4.tiles, f32[1,128]{1,0:T(1,128)S(1)} %get-tuple-element.28.gain, bf16[128,256]{1,0:T(8,128)(2,1)S(1)} %get-tuple-element.29.wkv, bf16[1024,128]{1,0:T(8,128)(2,1)S(1)} %get-tuple-element.30.q0, ...), custom_call_target="tpu_custom_call" | custom-call | flops 4294967296 | bytes 1114624 | tf_op jit(solution)/shard_map/near_row_tiles/pallas_call | solution.py:274
  29.4 0.0 collective-permute-done.3.tiles
  29.4 0.0 copy-done.7
  29.4 0.0 copy-done.8
  29.4 0.0 copy-start
  29.4 0.0 copy-start.1
  29.4 9.2 %far_row_tiles.1 = (bf16[1024,128]{1,0:T(8,128)(2,1)}, bf16[4,256]{1,0:T(4,128)(2,1)S(1)}, bf16[32,4,256]{2,1,0:T(4,128)(2,1)}) custom-call(bf16[3,1024,128]{2,1,0:T(8,128)(2,1)S(1)} %collective-permute-done.3.tiles, f32[1,128]{1,0:T(1,128)S(1)} %get-tuple-element.28.gain, bf16[128,256]{1,0:T(8,128)(2,1)S(1)} %get-tuple-element.29.wkv, ...), custom_call_target="tpu_custom_call" | custom-call | flops 6442450944 | bytes 5080064 | tf_op jit(solution)/shard_map/far_row_tiles/pallas_call | solution.py:274
  38.7 4.5 %all-to-all-start = ((bf16[32,4,256]{2,1,0:T(4,128)(2,1)}), bf16[32,4,256]{2,1,0:T(4,128)(2,1)S(1)}, u32[]{:S(2)}, u32[]{:S(2)}) async-start(bf16[32,4,256]{2,1,0:T(4,128)(2,1)} %get-tuple-element.43), calls=%async_computation | async-start | bytes 131072 | tf_op jit(solution)/shard_map/all_to_all | solution.py:385
  43.2 0.0 copy-start.6
  43.2 0.0 copy-done
  43.2 0.0 copy-done.1
  43.2 0.6 copy-done.6
  43.8 0.0 copy-start.2
  43.8 0.0 copy-start.3
  43.8 0.6 coarse_prepare.1
  44.5 7.5 %all-to-all-done = bf16[32,4,256]{2,1,0:T(4,128)(2,1)S(1)} async-done(((bf16[32,4,256]{2,1,0:T(4,128)(2,1)}), bf16[32,4,256]{2,1,0:T(4,128)(2,1)S(1)}, u32[]{:S(2)}, u32[]{:S(2)}) %all-to-all-start) | async-done | bytes 65568 | tf_op jit(solution)/shard_map/all_to_all | solution.py:385
  52.0 0.0 copy-done.2
  52.0 0.0 copy-done.3
  52.0 1.2 %coarse.1 = bf16[8,4,1024]{2,1,0:T(4,128)(2,1)S(1)} custom-call(f32[1,128]{1,0:T(1,128)S(1)} %get-tuple-element.42.factor, bf16[128,256]{1,0:T(8,128)(2,1)S(1)} %reshape.15.tokens, f32[1,1024]{1,0:T(1,128)S(1)} %get-tuple-element.44.gain, bf16[256,1024]{1,0:T(8,128)(2,1)S(1)} %copy-done, bf16[3,1024,128]{2,1,0:T(8,128)(2,1)S(1)} %copy-done.2, ...), custom_call_target="tpu_custom_call" | custom-call | bytes 1643008 | tf_op jit(solution)/shard_map/coarse/pallas_call | solution.py:274
  53.1 0.0 copy-start.5
  53.2 10.9 %all_to_all.10.parts = bf16[8,4,1024]{2,1,0:T(4,128)(2,1)S(1)} all-to-all(bf16[8,4,1024]{2,1,0:T(4,128)(2,1)S(1)} %coarse.1), channel_id=1, replica_groups=mesh['noise'=8,'row'=4,'col'=8] {'col'}, dimensions={0} | all-to-all | bytes 131072 | tf_op jit(solution)/shard_map/all_to_all | solution.py:414
  64.0 0.0 copy-done.5
  64.0 0.7 %coarse_out.1 = bf16[2,2,1024]{2,1,0:T(2,128)(2,1)} custom-call(bf16[8,4,1024]{2,1,0:T(4,128)(2,1)S(1)} %all_to_all.10.parts, f32[4,1024]{1,0:T(4,128)S(1)} %get-tuple-element.45.coarse_in, f32[1,1024]{1,0:T(1,128)S(1)} %bitcast.18), custom_call_target="tpu_custom_call" | custom-call | bytes 86016 | tf_op jit(solution)/shard_map/coarse_out/pallas_call | solution.py:274
  (1 shorter events, 0.0 us)
Async XLA Ops:
  0.6 6.7 %collective-permute-start.2 = (bf16[1024,128]{1,0:T(8,128)(2,1)}, bf16[1024,128]{1,0:T(8,128)(2,1)S(1)}, u32[]{:S(2)}, u32[]{:S(2)}) collective-permute-start(bf16[1024,128]{1,0:T(8,128)(2,1)} %bitcast.12), channel_id=1, source_target_pairs={{0,8},{16,24},{8,0},{24,16},{1,9},{17,25},{9,1},{25,17},{2,10},{18... | collective-permute-start | bytes 786440 | tf_op jit(solution)/shard_map/ppermute | solution.py:320
  0.7 13.3 %collective-permute-start.1 = (bf16[1024,128]{1,0:T(8,128)(2,1)}, bf16[1024,128]{1,0:T(8,128)(2,1)S(1)}, u32[]{:S(2)}, u32[]{:S(2)}) collective-permute-start(bf16[1024,128]{1,0:T(8,128)(2,1)} %bitcast.13), channel_id=1, source_target_pairs={{1,2},{3,4},{5,6},{7,0},{2,1},{4,3},{6,5},{0,7},{9,10},{11,12},{13... | collective-permute-start | bytes 786440 | tf_op jit(solution)/shard_map/ppermute | solution.py:322
  6.7 8.6 %collective-permute-start = (bf16[1024,128]{1,0:T(8,128)(2,1)}, bf16[1024,128]{1,0:T(8,128)(2,1)S(1)}, u32[]{:S(2)}, u32[]{:S(2)}) collective-permute-start(bf16[1024,128]{1,0:T(8,128)(2,1)} %bitcast.14), channel_id=1, source_target_pairs={{0,1},{2,3},{4,5},{6,7},{1,0},{3,2},{5,4},{7,6},{8,9},{10,11},{12,... | collective-permute-start | bytes 786440 | tf_op jit(solution)/shard_map/ppermute | solution.py:321
  15.2 1.0 %copy-start.4 = (bf16[32,32,128]{2,1,0:T(8,128)(2,1)S(1)}, bf16[32,32,128]{2,1,0:T(8,128)(2,1)}, u32[]{:S(2)}) copy-start(bf16[32,32,128]{2,1,0:T(8,128)(2,1)} %param.15) | copy-start | bytes 786436
  15.3 8.8 %collective-permute-start.4 = (bf16[2,1024,128]{2,1,0:T(8,128)(2,1)S(1)}, bf16[2,1024,128]{2,1,0:T(8,128)(2,1)S(1)}, u32[]{:S(2)}, u32[]{:S(2)}) collective-permute-start(bf16[2,1024,128]{2,1,0:T(8,128)(2,1)S(1)} %pad_maximum_fusion.1), channel_id=1, source_target_pairs={{0,8},{16,24},{8,0},{24,16},{1,9},{17,25},{9,1},{25,17},{2,10},{18... | collective-permute-start | bytes 1572872 | tf_op jit(solution)/shard_map/ppermute | solution.py:350
  16.3 13.1 %collective-permute-start.3 = (bf16[3,1024,128]{2,1,0:T(8,128)(2,1)S(1)}, bf16[3,1024,128]{2,1,0:T(8,128)(2,1)S(1)}, u32[]{:S(2)}, u32[]{:S(2)}) collective-permute-start(bf16[3,1024,128]{2,1,0:T(8,128)(2,1)S(1)} %pad_maximum_fusion), channel_id=1, source_target_pairs={{8,16},{24,32},{40,48},{56,0},{16,8},{32,24},{48,40},{0,56},{72,80... | collective-permute-start | bytes 2359304 | tf_op jit(solution)/shard_map/ppermute | solution.py:351
  24.1 5.3 %copy-start.7 = (bf16[512,256]{1,0:T(8,128)(2,1)S(1)}, bf16[512,256]{1,0:T(8,128)(2,1)}, u32[]{:S(2)}) copy-start(bf16[512,256]{1,0:T(8,128)(2,1)} %wmerge.1) | copy-start | bytes 786436
  24.1 5.3 %copy-start.8 = (bf16[128,128]{1,0:T(8,128)(2,1)S(1)}, bf16[128,128]{1,0:T(8,128)(2,1)}, u32[]{:S(2)}) copy-start(bf16[128,128]{1,0:T(8,128)(2,1)} %wout.2) | copy-start | bytes 98308
  29.4 13.8 %copy-start = (bf16[256,1024]{1,0:T(8,128)(2,1)S(1)}, bf16[256,1024]{1,0:T(8,128)(2,1)}, u32[]{:S(2)}) copy-start(bf16[256,1024]{1,0:T(8,128)(2,1)} %win.3) | copy-start | bytes 1572868
  29.4 13.8 %copy-start.1 = (f32[256,1024]{1,0:T(8,128)S(1)}, f32[256,1024]{1,0:T(8,128)}, u32[]{:S(2)}) copy-start(f32[256,1024]{1,0:T(8,128)} %ada.1) | copy-start | bytes 3145732
  38.7 13.3 %all-to-all-start = ((bf16[32,4,256]{2,1,0:T(4,128)(2,1)}), bf16[32,4,256]{2,1,0:T(4,128)(2,1)S(1)}, u32[]{:S(2)}, u32[]{:S(2)}) async-start(bf16[32,4,256]{2,1,0:T(4,128)(2,1)} %get-tuple-element.43), calls=%async_computation | async-start | bytes 131072 | tf_op jit(solution)/shard_map/all_to_all | solution.py:385
  43.2 0.7 %copy-start.6 = (f32[2]{0:T(128)S(1)}, f32[2]{0:T(128)}, u32[]{:S(2)}) copy-start(f32[2]{0:T(128)} %param.27) | copy-start | bytes 28
  43.8 8.1 %copy-start.2 = (bf16[3,1024,128]{2,1,0:T(8,128)(2,1)S(1)}, bf16[3,1024,128]{2,1,0:T(8,128)(2,1)}, u32[]{:S(2)}) copy-start(bf16[3,1024,128]{2,1,0:T(8,128)(2,1)} %wqkv.1) | copy-start | bytes 2359300
  43.8 8.1 %copy-start.3 = (bf16[128,1024]{1,0:T(8,128)(2,1)S(1)}, bf16[128,1024]{1,0:T(8,128)(2,1)}, u32[]{:S(2)}) copy-start(bf16[128,1024]{1,0:T(8,128)(2,1)} %wout.3) | copy-start | bytes 786436
  53.1 10.9 %copy-start.5 = (f32[1024]{0:T(1024)S(1)}, f32[1024]{0:T(1024)}, u32[]{:S(2)}) copy-start(f32[1024]{0:T(1024)} %param.29) | copy-start | bytes 12292

commit v5 on v4

--- a/solution.py
+++ b/solution.py
@@ -58,10 +58,11 @@
     xn = (rms_rows(x.astype(F32)) * (gain * valid)).astype(BF16)
     proj = mm(xn, wkv)
     k = head_rms(proj[:, :width]).astype(BF16)
-    v = proj[:, width:]
+    v = proj[:, width:].astype(BF16)
     low = low_lanes(v.shape)
-    v0 = jnp.where(low, v, valid).astype(BF16)
-    v1 = jnp.where(low, valid, v).astype(BF16)
+    flags = jnp.full(v.shape, valid, F32).astype(BF16)
+    v0 = jnp.where(low, v, flags)
+    v1 = jnp.where(low, flags, v)
     return xn, k, v0, v1
 
 
@@ -77,21 +78,14 @@
                 acc_ref[rows, :] += part
 
 
-def fetch(pairs, sems):
-    copies = [pltpu.make_async_copy(src, dst, sems.at[i]) for i, (src, dst) in enumerate(pairs)]
-    for copy in copies:
-        copy.start()
-    return copies
-
-
 def own_kernel(
     level,
-    scale_hbm,
-    x_hbm,
-    table_hbm,
-    ada_hbm,
-    wqkv_hbm,
-    post_hbm,
+    scale,
+    x,
+    table,
+    ada,
+    wqkv,
+    post,
     near_tile,
     q0,
     q1,
@@ -101,26 +95,8 @@
     cond_out,
     wkv_out,
     post_out,
-    scale,
-    x,
-    table,
-    ada,
-    wqkv,
-    sems,
 ):
-    copies = fetch(
-        (
-            (table_hbm, table),
-            (ada_hbm, ada),
-            (x_hbm, x),
-            (wqkv_hbm, wqkv),
-            (scale_hbm, scale),
-            (post_hbm, post_out),
-        ),
-        sems,
-    )
-    for copy in copies:
-        copy.wait()
+    post_out[...] = post[...]
     width = x.shape[1]
     cond = level_row(level, table)
     turned = table[...].T
@@ -264,11 +240,12 @@
     specs = {
         "s": pl.BlockSpec(memory_space=pltpu.SMEM),
         "v": pl.BlockSpec(memory_space=pltpu.VMEM),
-        "h": pl.BlockSpec(memory_space=pltpu.HBM),
+        "h": pl.BlockSpec(memory_space=pltpu.VMEM),
+        "t": pl.BlockSpec(memory_space=pltpu.SMEM),
     }
     moved = sum(a.size * a.dtype.itemsize for a in args)
     args = [
-        pltpu.with_memory_space_constraint(a, pltpu.HBM) if space == "h" else a
+        pltpu.with_memory_space_constraint(a, pltpu.HBM) if space in "ht" else a
         for a, space in zip(args, spaces)
     ]
     return pl.pallas_call(
@@ -320,7 +297,7 @@
     near_tile = lax.ppermute(x, "row", swaps(n_row, 0))
     col_a = lax.ppermute(x, "col", swaps(n_col, 0))
     col_b = lax.ppermute(x, "col", swaps(n_col, 1))
-    vmem, dma = pltpu.VMEM, pltpu.SemaphoreType.DMA
+    vmem = pltpu.VMEM
     accs = (shape((count, width), F32),) * 2
     q0, q1, own0, own1, gain, cond, wkv, post = call(
         own_kernel,
@@ -333,22 +310,14 @@
             shape((1, width), F32),
         ),
         (noise_level, fine_scale, x, cond_table, ada_fine, fine_qkv, fine_post[None], near_tile),
-        "shhhhhhv",
-        scratch=[
-            pltpu.SMEM(fine_scale.shape, F32),
-            vmem(x.shape, BF16),
-            vmem(cond_table.shape, F32),
-            vmem(ada_fine.shape, F32),
-            vmem(fine_qkv.shape, BF16),
-            dma((6,)),
-        ],
+        "sthhhhhv",
         flops=2 * tile_flops,
         name="own_tile",
     )
     held, col_a, col_b, gain = lax.optimization_barrier((x, col_a, col_b, gain))
     three = jnp.stack([held, col_a, col_b])
+    far = lax.ppermute(three, ("noise", "row"), far_pairs)
     near = lax.ppermute(jnp.stack([col_a, col_b]), "row", swaps(n_row, 0))
-    far = lax.ppermute(three, ("noise", "row"), far_pairs)
     col0, col1 = call(
         col_kernel,
         accs,

time: 65 us -> 65 us (level)
  no operation moved by 1% of the time
where the time goes in v5:
time: 65 us; the launch traced here: 64.7 us
  Pallas kernels  28.7 us (44%)
  starting transfers between devices  13.2 us (20%)
  blocking collectives  10.9 us (17%)
  waiting for transfers between devices  8.74 us (13%)
  local copies, waits for them, and re-layouts  1.49 us (2%)
  between operations  1.47 us (2%)
    pallas_call x7, Pallas kernels, call(): pl.pallas_call(kernel, out_shape=out_shape, in_specs=[specs[space] for sp...  28.7 us
    all_to_all x1, blocking collectives, body(): parts = lax.all_to_all(parts, 'col', 0, 0, tiled=True)  10.9 us
    all_to_all x1, waiting for transfers between devices, body(): tokens = lax.all_to_all(pooled_all, ('row', 'col'), 0, 0, tiled=True)  7.45 us
    ppermute x1, starting transfers between devices, body(): col_b = lax.ppermute(x, 'col', swaps(n_col, 1))  5.94 us
    all_to_all x1, starting transfers between devices, body(): tokens = lax.all_to_all(pooled_all, ('row', 'col'), 0, 0, tiled=True)  4.5 us
    ppermute x1, starting transfers between devices, body(): far = lax.ppermute(three, ('noise', 'row'), far_pairs)  2.59 us
    unnamed x18, local copies, waits for them, and re-layouts  1.47 us
  transfers between devices with their start and end apart: 6, of which 2 were waited for; matrix products, arithmetic and copies ran while one was open for 0% of the time, Pallas kernels for 27%

profile of v5, /device:TPU:2, one launch (start us, length us, event | category | flops | bytes accessed | tf_op | source)
XLA Modules:
  0.0 64.7 jit_solution(9951304268512745447)
XLA Ops:
  0.6 0.1 collective-permute-start.2
  0.7 5.9 %collective-permute-start.1 = (bf16[1024,128]{1,0:T(8,128)(2,1)}, bf16[1024,128]{1,0:T(8,128)(2,1)S(1)}, u32[]{:S(2)}, u32[]{:S(2)}) collective-permute-start(bf16[1024,128]{1,0:T(8,128)(2,1)} %bitcast.13), channel_id=1, source_target_pairs={{1,2},{3,4},{5,6},{7,0},{2,1},{4,3},{6,5},{0,7},{9,10},{11,12},{13... | collective-permute-start | bytes 786440 | tf_op jit(solution)/shard_map/ppermute | solution.py:299
  6.7 0.0 collective-permute-start
  7.3 0.0 collective-permute-done.2.near_tile
  7.3 6.6 %own_tile.1 = (bf16[1024,128]{1,0:T(8,128)(2,1)S(1)}, bf16[1024,128]{1,0:T(8,128)(2,1)S(1)}, f32[1024,128]{1,0:T(8,128)S(1)}, f32[1024,128]{1,0:T(8,128)S(1)}, f...) custom-call(s32[1]{0:T(128)S(6)} %copy.17.level, f32[2]{0:T(128)} %scale.1, ...), custom_call_target="tpu_custom_call" | custom-call | flops 4294967296 | bytes 762380 | tf_op jit(solution)/shard_map/own_tile/pallas_call | solution.py:251
  14.0 0.0 collective-permute-done.1.b
  14.0 1.3 %collective-permute-done.a = bf16[1024,128]{1,0:T(8,128)(2,1)S(1)} collective-permute-done((bf16[1024,128]{1,0:T(8,128)(2,1)}, bf16[1024,128]{1,0:T(8,128)(2,1)S(1)}, u32[]{:S(2)}, u32[]{:S(2)}) %collective-permute-start) | collective-permute-done | bytes 262176 | tf_op jit(solution)/shard_map/ppermute | solution.py:298
  15.2 0.0 copy-start.4
  15.2 0.1 pad_maximum_fusion.1
  15.3 0.1 collective-permute-start.4
  15.4 0.8 %copy-done.4 = bf16[32,32,128]{2,1,0:T(8,128)(2,1)S(1)} copy-done((bf16[32,32,128]{2,1,0:T(8,128)(2,1)S(1)}, bf16[32,32,128]{2,1,0:T(8,128)(2,1)}, u32[]{:S(2)}) %copy-start.4) | copy-done | bytes 262168
  16.2 0.1 pad_maximum_fusion
  16.3 2.6 %collective-permute-start.3 = (bf16[3,1024,128]{2,1,0:T(8,128)(2,1)S(1)}, bf16[3,1024,128]{2,1,0:T(8,128)(2,1)S(1)}, u32[]{:S(2)}, u32[]{:S(2)}) collective-permute-start(bf16[3,1024,128]{2,1,0:T(8,128)(2,1)S(1)} %pad_maximum_fusion), channel_id=1, source_target_pairs={{8,16},{24,32},{40,48},{56,0},{16,8},{32,24},{48,40},{0,56},{72,80... | collective-permute-start | bytes 2359304 | tf_op jit(solution)/shard_map/ppermute | solution.py:319
  18.9 5.2 %col_tiles.1 = (f32[1024,128]{1,0:T(8,128)S(1)}, f32[1024,128]{1,0:T(8,128)S(1)}) custom-call(bf16[1024,128]{1,0:T(8,128)(2,1)S(1)} %collective-permute-done.a, bf16[1024,128]{1,0:T(8,128)(2,1)S(1)} %collective-permute-done.1.b, f32[1,128]{1,0:T(1,128)S(1)} %get-tuple-element.28.gain, bf16[128,256]{1,0:T(8,128)(2,1)S(1)} %get-tuple-element.29.wkv, ...), custom_call_target="tpu_custom_call" | custom-call | flops 4294967296 | bytes 1114624 | tf_op jit(solution)/shard_map/col_tiles/pallas_call | solution.py:251
  24.1 0.0 copy-start.7
  24.1 0.0 copy-start.8
  24.1 0.0 collective-permute-done.4.tiles
  24.1 5.2 %near_row_tiles.1 = (f32[1024,128]{1,0:T(8,128)S(1)}, f32[1024,128]{1,0:T(8,128)S(1)}) custom-call(bf16[2,1024,128]{2,1,0:T(8,128)(2,1)S(1)} %collective-permute-done.4.tiles, f32[1,128]{1,0:T(1,128)S(1)} %get-tuple-element.28.gain, bf16[128,256]{1,0:T(8,128)(2,1)S(1)} %get-tuple-element.29.wkv, bf16[1024,128]{1,0:T(8,128)(2,1)S(1)} %get-tuple-element.30.q0, ...), custom_call_target="tpu_custom_call" | custom-call | flops 4294967296 | bytes 1114624 | tf_op jit(solution)/shard_map/near_row_tiles/pallas_call | solution.py:251
  29.3 0.0 collective-permute-done.3.tiles
  29.3 0.0 copy-done.7
  29.3 0.0 copy-done.8
  29.3 0.0 copy-start
  29.3 0.0 copy-start.1
  29.4 9.2 %far_row_tiles.1 = (bf16[1024,128]{1,0:T(8,128)(2,1)}, bf16[4,256]{1,0:T(4,128)(2,1)S(1)}, bf16[32,4,256]{2,1,0:T(4,128)(2,1)}) custom-call(bf16[3,1024,128]{2,1,0:T(8,128)(2,1)S(1)} %collective-permute-done.3.tiles, f32[1,128]{1,0:T(1,128)S(1)} %get-tuple-element.28.gain, bf16[128,256]{1,0:T(8,128)(2,1)S(1)} %get-tuple-element.29.wkv, ...), custom_call_target="tpu_custom_call" | custom-call | flops 6442450944 | bytes 5080064 | tf_op jit(solution)/shard_map/far_row_tiles/pallas_call | solution.py:251
  38.6 4.5 %all-to-all-start = ((bf16[32,4,256]{2,1,0:T(4,128)(2,1)}), bf16[32,4,256]{2,1,0:T(4,128)(2,1)S(1)}, u32[]{:S(2)}, u32[]{:S(2)}) async-start(bf16[32,4,256]{2,1,0:T(4,128)(2,1)} %get-tuple-element.43), calls=%async_computation | async-start | bytes 131072 | tf_op jit(solution)/shard_map/all_to_all | solution.py:354
  43.1 0.0 copy-start.6
  43.1 0.0 copy-done
  43.1 0.0 copy-done.1
  43.1 0.6 copy-done.6
  43.7 0.0 copy-start.2
  43.7 0.0 copy-start.3
  43.7 0.6 coarse_prepare.1
  44.4 7.5 %all-to-all-done = bf16[32,4,256]{2,1,0:T(4,128)(2,1)S(1)} async-done(((bf16[32,4,256]{2,1,0:T(4,128)(2,1)}), bf16[32,4,256]{2,1,0:T(4,128)(2,1)S(1)}, u32[]{:S(2)}, u32[]{:S(2)}) %all-to-all-start) | async-done | bytes 65568 | tf_op jit(solution)/shard_map/all_to_all | solution.py:354
  51.8 0.0 copy-done.2
  51.9 0.0 copy-done.3
  51.9 1.2 %coarse.1 = bf16[8,4,1024]{2,1,0:T(4,128)(2,1)S(1)} custom-call(f32[1,128]{1,0:T(1,128)S(1)} %get-tuple-element.42.factor, bf16[128,256]{1,0:T(8,128)(2,1)S(1)} %reshape.15.tokens, f32[1,1024]{1,0:T(1,128)S(1)} %get-tuple-element.44.gain, bf16[256,1024]{1,0:T(8,128)(2,1)S(1)} %copy-done, bf16[3,1024,128]{2,1,0:T(8,128)(2,1)S(1)} %copy-done.2, ...), custom_call_target="tpu_custom_call" | custom-call | bytes 1643008 | tf_op jit(solution)/shard_map/coarse/pallas_call | solution.py:251
  53.1 0.0 copy-start.5
  53.1 10.9 %all_to_all.10.parts = bf16[8,4,1024]{2,1,0:T(4,128)(2,1)S(1)} all-to-all(bf16[8,4,1024]{2,1,0:T(4,128)(2,1)S(1)} %coarse.1), channel_id=1, replica_groups=mesh['noise'=8,'row'=4,'col'=8] {'col'}, dimensions={0} | all-to-all | bytes 131072 | tf_op jit(solution)/shard_map/all_to_all | solution.py:383
  64.0 0.0 copy-done.5
  64.0 0.7 %coarse_out.1 = bf16[2,2,1024]{2,1,0:T(2,128)(2,1)} custom-call(bf16[8,4,1024]{2,1,0:T(4,128)(2,1)S(1)} %all_to_all.10.parts, f32[4,1024]{1,0:T(4,128)S(1)} %get-tuple-element.45.coarse_in, f32[1,1024]{1,0:T(1,128)S(1)} %bitcast.18), custom_call_target="tpu_custom_call" | custom-call | bytes 86016 | tf_op jit(solution)/shard_map/coarse_out/pallas_call | solution.py:251
  (1 shorter events, 0.0 us)
Async XLA Ops:
  0.6 6.7 %collective-permute-start.2 = (bf16[1024,128]{1,0:T(8,128)(2,1)}, bf16[1024,128]{1,0:T(8,128)(2,1)S(1)}, u32[]{:S(2)}, u32[]{:S(2)}) collective-permute-start(bf16[1024,128]{1,0:T(8,128)(2,1)} %bitcast.12), channel_id=1, source_target_pairs={{0,8},{16,24},{8,0},{24,16},{1,9},{17,25},{9,1},{25,17},{2,10},{18... | collective-permute-start | bytes 786440 | tf_op jit(solution)/shard_map/ppermute | solution.py:297
  0.7 13.2 %collective-permute-start.1 = (bf16[1024,128]{1,0:T(8,128)(2,1)}, bf16[1024,128]{1,0:T(8,128)(2,1)S(1)}, u32[]{:S(2)}, u32[]{:S(2)}) collective-permute-start(bf16[1024,128]{1,0:T(8,128)(2,1)} %bitcast.13), channel_id=1, source_target_pairs={{1,2},{3,4},{5,6},{7,0},{2,1},{4,3},{6,5},{0,7},{9,10},{11,12},{13... | collective-permute-start | bytes 786440 | tf_op jit(solution)/shard_map/ppermute | solution.py:299
  6.7 8.6 %collective-permute-start = (bf16[1024,128]{1,0:T(8,128)(2,1)}, bf16[1024,128]{1,0:T(8,128)(2,1)S(1)}, u32[]{:S(2)}, u32[]{:S(2)}) collective-permute-start(bf16[1024,128]{1,0:T(8,128)(2,1)} %bitcast.14), channel_id=1, source_target_pairs={{0,1},{2,3},{4,5},{6,7},{1,0},{3,2},{5,4},{7,6},{8,9},{10,11},{12,... | collective-permute-start | bytes 786440 | tf_op jit(solution)/shard_map/ppermute | solution.py:298
  15.2 1.0 %copy-start.4 = (bf16[32,32,128]{2,1,0:T(8,128)(2,1)S(1)}, bf16[32,32,128]{2,1,0:T(8,128)(2,1)}, u32[]{:S(2)}) copy-start(bf16[32,32,128]{2,1,0:T(8,128)(2,1)} %param.15) | copy-start | bytes 786436
  15.3 8.8 %collective-permute-start.4 = (bf16[2,1024,128]{2,1,0:T(8,128)(2,1)S(1)}, bf16[2,1024,128]{2,1,0:T(8,128)(2,1)S(1)}, u32[]{:S(2)}, u32[]{:S(2)}) collective-permute-start(bf16[2,1024,128]{2,1,0:T(8,128)(2,1)S(1)} %pad_maximum_fusion.1), channel_id=1, source_target_pairs={{0,8},{16,24},{8,0},{24,16},{1,9},{17,25},{9,1},{25,17},{2,10},{18... | collective-permute-start | bytes 1572872 | tf_op jit(solution)/shard_map/ppermute | solution.py:320
  16.3 13.0 %collective-permute-start.3 = (bf16[3,1024,128]{2,1,0:T(8,128)(2,1)S(1)}, bf16[3,1024,128]{2,1,0:T(8,128)(2,1)S(1)}, u32[]{:S(2)}, u32[]{:S(2)}) collective-permute-start(bf16[3,1024,128]{2,1,0:T(8,128)(2,1)S(1)} %pad_maximum_fusion), channel_id=1, source_target_pairs={{8,16},{24,32},{40,48},{56,0},{16,8},{32,24},{48,40},{0,56},{72,80... | collective-permute-start | bytes 2359304 | tf_op jit(solution)/shard_map/ppermute | solution.py:319
  24.1 5.2 %copy-start.7 = (bf16[512,256]{1,0:T(8,128)(2,1)S(1)}, bf16[512,256]{1,0:T(8,128)(2,1)}, u32[]{:S(2)}) copy-start(bf16[512,256]{1,0:T(8,128)(2,1)} %wmerge.1) | copy-start | bytes 786436
  24.1 5.2 %copy-start.8 = (bf16[128,128]{1,0:T(8,128)(2,1)S(1)}, bf16[128,128]{1,0:T(8,128)(2,1)}, u32[]{:S(2)}) copy-start(bf16[128,128]{1,0:T(8,128)(2,1)} %wout.2) | copy-start | bytes 98308
  29.3 13.8 %copy-start = (bf16[256,1024]{1,0:T(8,128)(2,1)S(1)}, bf16[256,1024]{1,0:T(8,128)(2,1)}, u32[]{:S(2)}) copy-start(bf16[256,1024]{1,0:T(8,128)(2,1)} %win.3) | copy-start | bytes 1572868
  29.3 13.8 %copy-start.1 = (f32[256,1024]{1,0:T(8,128)S(1)}, f32[256,1024]{1,0:T(8,128)}, u32[]{:S(2)}) copy-start(f32[256,1024]{1,0:T(8,128)} %ada.3) | copy-start | bytes 3145732
  38.6 13.3 %all-to-all-start = ((bf16[32,4,256]{2,1,0:T(4,128)(2,1)}), bf16[32,4,256]{2,1,0:T(4,128)(2,1)S(1)}, u32[]{:S(2)}, u32[]{:S(2)}) async-start(bf16[32,4,256]{2,1,0:T(4,128)(2,1)} %get-tuple-element.43), calls=%async_computation | async-start | bytes 131072 | tf_op jit(solution)/shard_map/all_to_all | solution.py:354
  43.1 0.7 %copy-start.6 = (f32[2]{0:T(128)S(1)}, f32[2]{0:T(128)}, u32[]{:S(2)}) copy-start(f32[2]{0:T(128)} %param.27) | copy-start | bytes 28
  43.7 8.1 %copy-start.2 = (bf16[3,1024,128]{2,1,0:T(8,128)(2,1)S(1)}, bf16[3,1024,128]{2,1,0:T(8,128)(2,1)}, u32[]{:S(2)}) copy-start(bf16[3,1024,128]{2,1,0:T(8,128)(2,1)} %wqkv.3) | copy-start | bytes 2359300
  43.7 8.1 %copy-start.3 = (bf16[128,1024]{1,0:T(8,128)(2,1)S(1)}, bf16[128,1024]{1,0:T(8,128)(2,1)}, u32[]{:S(2)}) copy-start(bf16[128,1024]{1,0:T(8,128)(2,1)} %wout.3) | copy-start | bytes 786436
  53.1 10.9 %copy-start.5 = (f32[1024]{0:T(1024)S(1)}, f32[1024]{0:T(1024)}, u32[]{:S(2)}) copy-start(f32[1024]{0:T(1024)} %param.29) | copy-start | bytes 12292
